TPU v7x, 256 devices: a whole 4x4x8 slice. The times are simulated.
256 devices in a mesh: vid: 128 (over z, y, x_lo, core), aud: 2 (over x_hi).
Axes of the slice: x: 4 (x_hi: 2, x_lo: 2; x = x_hi * 2 + x_lo), y: 4, z: 8, core: 2. Of those that a mesh axis runs over, the one named last changes fastest.
Arguments:
- q_video: bfloat16 [32768, 1536], P('vid', 'aud'), may hold values from -240 to 240
- video_key_rows: bfloat16 [32768, 1536], P('vid', 'aud'), may hold values from -6 to 6
- video_value_rows: bfloat16 [32768, 1536], P('vid', 'aud'), may hold values from -6 to 6
- g_video: bfloat16 [32768, 1536], P('vid', 'aud'), may hold values from -6 to 6
- q_audio: bfloat16 [8192, 1536], P(('vid', 'aud')), may hold values from -240 to 240
- k_audio: bfloat16 [8192, 1536], P(('vid', 'aud')), may hold values from -6 to 6
- v_audio: bfloat16 [8192, 1536], P(('vid', 'aud')), may hold values from -6 to 6
- g_audio: bfloat16 [8192, 1536], P(('vid', 'aud')), may hold values from -6 to 6
- window: int32 [512, 2], replicated, may hold values from 0 to 127, as said below
- audio_len: int32 [128], replicated, may hold values from 1 to 64
Outputs:
- out_video: bfloat16 [32768, 1536], P('vid', 'aud')
- out_audio: bfloat16 [8192, 1536], P(('vid', 'aud'))
- dq_video: bfloat16 [32768, 1536], P('vid', 'aud')
- dk_video: bfloat16 [32768, 1536], P('vid', 'aud')
- dv_video: bfloat16 [32768, 1536], P('vid', 'aud')
- dq_audio: bfloat16 [8192, 1536], P(('vid', 'aud'))
- dk_audio: bfloat16 [8192, 1536], P(('vid', 'aud'))
- dv_audio: bfloat16 [8192, 1536], P(('vid', 'aud'))
Inputs may be any that keep to these rules, and one draw needn't show every extreme that they name: window[i] = (start, count) with 1 <= count <= 3 (3 is reached in every draw), start <= i // 4 < start + count, and start + count <= 128.
All inputs are finite; a program needn't handle non-finite values.
Results may differ from a plain program's by a relative error of at most 0.0095.
Values may be sent and summed in bfloat16 or wider, within the bound.
No kernel may reach another device: no remote copies, remote signals or barrier semaphores. Data moves between devices by JAX's collectives and lax.ppermute only.
A program may use at most 64 MiB of HBM per device.

v0:
```python
import functools

import jax
import jax.numpy as jnp
from jax import lax
from jax.experimental import pallas as pl
from jax.experimental.pallas import tpu as pltpu
from jax.sharding import PartitionSpec as P


HD = 64
BLK = 64
WMAX = 3
PAIR = 2 * HD
NEG = -1e30
BF = jnp.bfloat16
F32 = jnp.float32


NPOS = 6
KEYS = NPOS * BLK
GROUP = 8


def nt(x, y):
    return lax.dot_general(x, y, (((1,), (1,)), ((), ())), preferred_element_type=F32)


def nn(x, y):
    return lax.dot_general(x, y, (((1,), (0,)), ((), ())), preferred_element_type=F32)


def coords():
    vid, aud = lax.axis_index("vid"), lax.axis_index("aud")
    return vid >> 1, vid & 1, aud


def head_part(x, e):
    lane = lax.broadcasted_iota(jnp.int32, x.shape, 1)
    return jnp.where((lane < HD) if e == 0 else (lane >= HD), x, jnp.zeros_like(x))


def load_kernel(*refs):
    srcs, dst, sems = refs[:4], refs[4], refs[5]
    copies = [pltpu.make_async_copy(src, dst.at[n], sems.at[n]) for n, src in enumerate(srcs)]
    for copy in copies:
        copy.start()
    for copy in copies:
        copy.wait()


def pack_kernel(len_ref, mine, *refs):
    other, (keep, send, mask) = refs[:4], refs[4:]
    c, r, a = coords()
    half, quarter = keep.shape[2], keep.shape[3]
    row = lax.broadcasted_iota(jnp.int32, (half, quarter), 0) + a * half
    for slot, arrays in ((r, [mine.at[n] for n in range(4)]), (1 - r, other)):
        valid = row < len_ref[2 * c + slot]
        mask[slot] = jnp.where(valid, 1.0, 0.0)
        for n, ref in enumerate(arrays):

            def part(which, core):
                col = pl.multiple_of((2 * which + core) * quarter, 128)
                x = ref[:, pl.ds(col, quarter)]
                if n == 0:
                    x = x * jnp.asarray(HD**-0.5, BF)
                if n == 1:
                    x = jnp.where(valid, x, jnp.zeros_like(x))
                return x

            keep[n, slot] = part(a, r)
            send[n, slot] = part(1 - a, r)


def piece_rows():
    c, _, a = coords()
    half = BLK // 2
    side = 2 - 2 * (c & 1)
    starts = []
    for place, part in ((1, a), (1, 1 - a), (side, a), (side, 1 - a), (2 - side, a), (2 - side, 1 - a)):
        first = place * 2 * BLK + part * half
        starts.append([pl.multiple_of(first + core * BLK, half) for core in range(2)])
    return starts


def gather_audio(pieces, arrays, dst):
    half = BLK // 2
    for ref, firsts in zip(pieces, piece_rows()):
        for core, first in enumerate(firsts):
            for n, k in enumerate(arrays):
                dst[n, pl.ds(first, half), :] = ref[k, core]


def scatter_audio(sources, pieces):
    half = BLK // 2
    for ref, firsts in zip(pieces, piece_rows()):
        for core, first in enumerate(firsts):
            for n, src in enumerate(sources):
                ref[n, core] = src[n % 2, pl.ds(first, half), :]


def pair_cols(h, quarter):
    _, r, _ = coords()
    col = pl.multiple_of(h * PAIR, PAIR)
    return pl.ds(col, PAIR), pl.ds(pl.multiple_of(r * quarter + col, PAIR), PAIR)


def window_bounds(win_ref, c, stretch, shape, axis):
    block = lax.broadcasted_iota(jnp.int32, shape, axis) // BLK
    lo = jnp.zeros(shape, jnp.int32)
    hi = jnp.zeros(shape, jnp.int32)
    for b in range(4):
        start = win_ref[0, 8 * c + 4 * stretch + b] - (2 * c - 2)
        count = win_ref[1, 8 * c + 4 * stretch + b]
        lo = jnp.where(block == b, start, lo)
        hi = jnp.where(block == b, start + count, hi)
    return lo, hi


def window_of(win_ref, stretch, b):
    c, _, _ = coords()
    block = 8 * c + 4 * stretch + b
    return win_ref[0, block] - (2 * c - 2), win_ref[1, block]


def block_bias(win_ref, len_ref, bias):
    c, r, _ = coords()
    row = lax.broadcasted_iota(jnp.int32, bias.shape[1:], 0)
    for i, stretch in enumerate((r, 1 - r)):
        for b in range(4):
            start, count = window_of(win_ref, stretch, b)
            keep = row < count * BLK
            if len_ref is not None:
                length = jnp.zeros(row.shape, jnp.int32)
                for j in range(WMAX):
                    block = jnp.clip(2 * c - 2 + start + j, 0, len_ref.shape[0] - 1)
                    length = jnp.where(row // BLK == j, len_ref[block], length)
                keep = keep & (row % BLK < length)
            bias[4 * i + b] = jnp.where(keep, 0.0, NEG)


def both_heads(x):
    return jnp.concatenate([head_part(x, 0), head_part(x, 1)], axis=0)


def own_heads(x):
    lane = lax.broadcasted_iota(jnp.int32, (BLK, PAIR), 1)
    return jnp.where(lane < HD, x[:BLK], x[BLK:])


def block_groups(r):
    blocks = [(i, stretch, b) for b in range(4) for i, stretch in enumerate((r, 1 - r))]
    return [blocks[n : n + GROUP] for n in range(0, 8, GROUP)]


def tn(x, y):
    return lax.dot_general(x, y, (((0,), (0,)), ((), ())), preferred_element_type=F32)


def group_places(c):
    side = 2 - 2 * (c & 1)
    return 1, side, 2 - side


def group_bias(win_ref, groups, bias):
    c, r, _ = coords()
    places = group_places(c)
    shape = bias.shape[1:]
    lane = lax.broadcasted_iota(jnp.int32, shape, 1)
    place = jnp.zeros(shape, jnp.int32)
    for n, group in enumerate(groups):
        place = jnp.where(lane // PAIR == n, 2 * places[group], place)
    place = place + (lane % PAIR) // BLK
    for i, stretch in enumerate((r, 1 - r)):
        lo, hi = window_bounds(win_ref, c, stretch, shape, 0)
        bias[i] = jnp.where((place >= lo) & (place < hi), 0.0, NEG)


def pair_stats(x, y):
    m = jnp.maximum(x[0:2], y[0:2])
    wx, wy = jnp.exp(x[0:2] - m), jnp.exp(y[0:2] - m)
    total = wx + wy
    lse, delta = m + jnp.log(total), (wx * x[2:4] + wy * y[2:4]) / total
    return jnp.concatenate([lse, delta, lse, delta], axis=0)


def stats_kernel(groups, win_ref, *refs):
    count = len(groups)
    pieces, refs = refs[: 2 * count], refs[2 * count :]
    video, refs = ((refs[0], refs[1]), (refs[2], refs[3])), refs[4:]
    stat_ref, audio, bias = refs[-3:]
    _, _, a = coords()
    half, quarter = BLK // 2, audio.shape[2]
    group_bias(win_ref, groups, bias)
    for n in range(count):
        for ref, part in ((pieces[2 * n], a), (pieces[2 * n + 1], 1 - a)):
            for core in range(2):
                first = pl.multiple_of(n * PAIR + core * BLK + part * half, half)
                for k in range(2):
                    audio[k, pl.ds(first, half), :] = ref[k, core]

    @pl.loop(0, quarter // PAIR, unroll=True)
    def _(h):
        cols, wide_cols = pair_cols(h, quarter)
        queries, cot = audio[0, :, cols], audio[1, :, cols]
        work = []
        for e in range(2):
            s = [nt(head_part(k_ref[:, wide_cols], e), queries) + bias[i] for i, (k_ref, _) in enumerate(video)]
            work.append((s, [nt(head_part(v_ref[:, wide_cols], e), cot) for _, v_ref in video]))
        lses, deltas = [], []
        for s, dp in work:
            m = jnp.maximum(*[jnp.max(x, axis=0, keepdims=True) for x in s])
            ex = [jnp.exp(x - m) for x in s]
            total = sum(jnp.sum(x, axis=0, keepdims=True) for x in ex)
            lses.append(m + jnp.log(total))
            deltas.append(sum(jnp.sum(x * y, axis=0, keepdims=True) for x, y in zip(ex, dp)) / total)
        rows = jnp.concatenate(lses + deltas + lses + deltas, axis=0)
        if count == 1:
            rows = jnp.concatenate([pair_stats(refs[0][h][:, :PAIR], refs[1][h][:, PAIR:]), rows], axis=1)
        stat_ref[h] = rows


def merge_stats(chips, own_a, own_b, by_a, by_b, by_q2):
    c, _, _ = coords()
    even = (c & 1) == 0
    has_b = jnp.where(even, c >= 2, c + 2 < chips)
    has_q2 = jnp.where(even, c + 2 < chips, c >= 2)

    def part(x, k, there=None):
        x = x[:, k * PAIR : (k + 1) * PAIR]
        return (x[0:2] if there is None else jnp.where(there, x[0:2], NEG)), x[2:4]

    merged = []
    for group in (
        (part(own_a, 0), part(by_a, 1), part(by_b, 1, has_b)),
        (part(own_a, 1), part(by_a, 0), part(by_q2, 1, has_q2)),
        (part(own_b, 1), part(by_b, 0, has_b)),
    ):
        m = functools.reduce(jnp.maximum, [lse for lse, _ in group])
        ws = [jnp.exp(lse - m) for lse, _ in group]
        total = sum(ws)
        merged.append((m + jnp.log(total), sum(wt * d for wt, (_, d) in zip(ws, group)) / total))
    return merged


def va_kernel(win_ref, len_ref, *refs):
    pieces = refs[:6]
    video = ((refs[6], refs[7]), (refs[8], refs[9]))
    outs = ((refs[10], refs[11]), (refs[12], refs[13]))
    kv_grads, audio, bias, grads = refs[14:]
    _, r, _ = coords()
    quarter = audio.shape[2]
    block_bias(win_ref, len_ref, bias)
    gather_audio(pieces, (2, 3), audio)
    scale = jnp.asarray(HD**-0.5, BF)

    @pl.loop(0, quarter // PAIR)
    def _(h):
        cols, wide_cols = pair_cols(h, quarter)
        grads[...] = jnp.zeros(grads.shape, F32)
        for group in block_groups(r):
            work = []
            for i, stretch, b in group:
                start, _ = window_of(win_ref, stretch, b)
                span = pl.ds(pl.multiple_of(start * BLK, BLK), WMAX * BLK)
                rows = slice(b * BLK, (b + 1) * BLK)
                q = both_heads(video[i][0][rows, wide_cols] * scale)
                g = both_heads(video[i][1][rows, wide_cols])
                keys, values = audio[0, span, cols], audio[1, span, cols]
                s = nt(keys, q) + bias[4 * i + b]
                dp = nt(values, g)
                work.append((i, rows, span, q, g, keys, values, s, dp))
            done = []
            for i, rows, span, q, g, keys, values, s, dp in work:
                ex = jnp.exp(s - jnp.max(s, axis=0, keepdims=True))
                inv = 1.0 / jnp.sum(ex, axis=0, keepdims=True)
                delta = jnp.sum(ex * dp, axis=0, keepdims=True) * inv
                p = ex * inv
                pb = p.astype(BF)
                ds = (p * (dp - delta)).astype(BF)
                done.append((i, rows, span, nn(ds, q), nn(pb, g), tn(pb, values), tn(ds, keys)))
            for i, rows, span, dk, dv, out, dq in done:
                grads[0, span, :] += dk
                grads[1, span, :] += dv
                outs[i][0][rows, cols] = own_heads(out).astype(BF)
                outs[i][1][rows, cols] = (own_heads(dq) * HD**-0.5).astype(BF)
        for n in range(2):
            kv_grads[n, :, cols] = grads[n].astype(BF)


def av_kernel(chips, win_ref, *refs):
    pieces = refs[:6]
    video = ((refs[6], refs[7]), (refs[8], refs[9]))
    stats, kv_grads = refs[10:15], refs[15]
    outs = ((refs[16], refs[17]), (refs[18], refs[19]))
    back = refs[20:26]
    audio, bias, grads, rowstat, qo_grads = refs[26:]
    c, r, _ = coords()
    quarter = audio.shape[2]
    block_bias(win_ref, None, bias)
    gather_audio(pieces, (0, 1), audio)

    @pl.loop(0, quarter // PAIR)
    def _(h):
        cols, wide_cols = pair_cols(h, quarter)
        for place, merged in zip(group_places(c), merge_stats(chips, *[ref[h] for ref in stats])):
            for n, x in enumerate(merged):
                wide = [jnp.broadcast_to(x[e : e + 1], (HD, PAIR)) for e in range(2)]
                rowstat[n, pl.ds(place * PAIR, PAIR), :] = jnp.concatenate(wide, axis=0).T
        grads[...] = jnp.zeros(grads.shape, F32)
        for group in block_groups(r):
            work = []
            for i, stretch, b in group:
                start, _ = window_of(win_ref, stretch, b)
                span = pl.ds(pl.multiple_of(start * BLK, BLK), WMAX * BLK)
                rows = slice(b * BLK, (b + 1) * BLK)
                keys = both_heads(video[i][0][rows, wide_cols])
                values = both_heads(video[i][1][rows, wide_cols])
                q, g = audio[0, span, cols], audio[1, span, cols]
                s = nt(q, keys) + bias[4 * i + b]
                dp = nt(g, values)
                work.append((i, rows, span, keys, values, q, g, s, dp))
            done = []
            for i, rows, span, keys, values, q, g, s, dp in work:
                p = jnp.exp(s - rowstat[0, span, :])
                pb = p.astype(BF)
                ds = (p * (dp - rowstat[1, span, :])).astype(BF)
                done.append((i, rows, span, nn(ds, keys), nn(pb, values), tn(ds, q), tn(pb, g)))
            for i, rows, span, dq, out, dk, dv in done:
                grads[0, span, :] += dq
                grads[1, span, :] += out
                outs[i][0][rows, cols] = own_heads(dk).astype(BF)
                outs[i][1][rows, cols] = own_heads(dv).astype(BF)
        qo_grads[0, :, cols] = (grads[0] * HD**-0.5).astype(BF)
        qo_grads[1, :, cols] = grads[1].astype(BF)

    scatter_audio((kv_grads, kv_grads, qo_grads, qo_grads), back)


def sum_kernel(mask, keep, by_aud, by_a, by_ax, by_b, by_bx, after, mine, other):
    _, r, a = coords()
    for slot, out in ((r, mine), (1 - r, other)):
        for part, parts in ((a, (keep, by_a, by_b)), (1 - a, (by_aud, by_ax, by_bx))):
            for n in range(4):
                x = sum(ref[n, slot].astype(F32) for ref in parts)
                if n == 3:
                    x = jnp.where(mask[slot] > 0.0, x, 0.0)
                out[n, part] = x.astype(BF)


def join_audio_kernel(mine, other, *outs):
    _, r, _ = coords()
    quarter = mine.shape[3]
    for n, out in enumerate(outs):
        for part in range(2):
            for core, ref in ((r, mine), (1 - r, other)):
                col = pl.multiple_of((2 * part + core) * quarter, 128)
                out[:, pl.ds(col, quarter)] = ref[n, part]


def join_video_kernel(*refs):
    _, r, _ = coords()
    quarter = refs[0].shape[1]
    for own, far, out in zip(refs[:4], refs[4:8], refs[8:12]):
        for core, src in ((r, own), (1 - r, far)):
            out[:, pl.ds(pl.multiple_of(core * quarter, PAIR), quarter)] = src[...]
    refs[12][...] = jnp.zeros(refs[12].shape, F32)


def cost(flops, transcendentals, nbytes):
    return pl.CostEstimate(flops=flops, transcendentals=transcendentals, bytes_accessed=nbytes)


def make_body(mesh):
    nv = mesh.shape["vid"]
    chips = nv // 2
    everyone = [(v, a) for v in range(nv) for a in range(2)]

    def perm(move):
        pairs = []
        for v, a in everyone:
            w, b = move(v, a)
            if 0 <= w < nv:
                pairs.append((2 * v + a, 2 * w + b))
        return pairs

    def diagonal(v):
        return 2 * ((((v >> 1) + 1) ^ 1) - 1) + (v & 1)

    moves = {
        "core": perm(lambda v, a: (v ^ 1, a)),
        "aud": perm(lambda v, a: (v, 1 - a)),
        "A": perm(lambda v, a: (v ^ 2, a)),
        "Ax": perm(lambda v, a: (v ^ 2, 1 - a)),
        "B": perm(lambda v, a: (diagonal(v), a)),
        "Bx": perm(lambda v, a: (diagonal(v), 1 - a)),
        "Q2": perm(lambda v, a: (v + 4 if v & 2 else v - 4, a)),
    }

    def move(x, name):
        return lax.ppermute(x, ("vid", "aud"), moves[name])

    def step(q_v, k_v, v_v, g_v, q_a, k_a, v_a, g_a, window, audio_len):
        rows, width = q_v.shape
        quarter = width // 2
        half = q_a.shape[0]
        steps = quarter // PAIR
        window = window.T
        shape = jax.ShapeDtypeStruct

        smem = pl.BlockSpec(memory_space=pltpu.SMEM)
        whole = pl.BlockSpec(memory_space=pltpu.VMEM)
        hbm = pl.BlockSpec(memory_space=pltpu.HBM)

        def call(kernel, name, ins, outs, args, scratch=(), est=None):
            params = dict(
                name=name,
                out_shape=[o for _, o in outs],
                cost_estimate=est,
                compiler_params=pltpu.CompilerParams(vmem_limit_bytes=24 << 20),
            )
            outs = [s for s, _ in outs]
            return pl.pallas_call(kernel, in_specs=ins, out_specs=outs, scratch_shapes=list(scratch), **params)(*args)

        audio = (q_a, g_a, k_a, v_a)
        audio_other = [move(x, "core") for x in audio]
        piece = shape((4, 2, half, quarter), BF)
        stack = shape((4, half, 2 * width), BF)
        (mine,) = call(
            load_kernel,
            "load",
            [hbm] * 4,
            [(whole, stack)],
            [pltpu.with_memory_space_constraint(x, pltpu.HBM) for x in audio],
            scratch=(pltpu.SemaphoreType.DMA((4,)),),
            est=cost(0, 0, 800000),
        )
        keep, send, mask = call(
            pack_kernel,
            "pack",
            [smem] + [whole] * 5,
            [(whole, piece)] * 2 + [(whole, shape((2, half, quarter), F32))],
            (audio_len, mine, *audio_other),
            est=cost(0, 0, 1600000),
        )
        pieces = [keep, move(send, "aud"), move(keep, "A"), move(send, "Ax")]
        pieces += [move(keep, "B"), move(send, "Bx")]
        k_f, v_f, q_f, g_f = [move(x, "core") for x in (k_v, v_v, q_v, g_v)]

        audio_scratch = pltpu.VMEM((2, KEYS, quarter), BF)
        grad_scratch = pltpu.VMEM((2, KEYS, PAIR), F32)
        bias_scratch = pltpu.VMEM((8, WMAX * BLK, PAIR), F32)
        pairs = 2 * steps * 2 * rows * KEYS

        stat = shape((steps, 8, 2 * PAIR), F32)

        def find_stats(groups, name, before):
            lanes = len(groups) * PAIR
            (found,) = call(
                lambda *refs: stats_kernel(groups, *refs),
                name,
                [smem] + [whole] * (2 * len(groups) + 4 + len(before)),
                [(whole, stat)],
                (window, *[pieces[2 * g + n] for g in groups for n in range(2)], k_v, v_v, k_f, v_f, *before),
                scratch=(pltpu.VMEM((2, lanes, quarter), BF), pltpu.VMEM((2, rows, lanes), F32)),
                est=cost(4 * HD * pairs * lanes // KEYS, pairs * lanes // KEYS, 2000000),
            )
            return found

        stats_a = find_stats((0, 1), "stats_a", ())
        by_a = move(stats_a, "A")
        stats_b = find_stats((2,), "stats_b", (stats_a, by_a))
        by_b, by_q2 = move(stats_b, "B"), move(stats_b, "Q2")

        full, part = shape((rows, width), BF), shape((rows, quarter), BF)
        out_own, dq_own, out_far, dq_far, kv_grads = call(
            va_kernel,
            "va",
            [smem, smem] + [whole] * 10,
            [(whole, part)] * 4 + [(whole, shape((2, KEYS, quarter), BF))],
            (window, audio_len, *pieces, *[pltpu.with_memory_space_constraint(x, pltpu.VMEM) for x in (q_v, g_v, q_f, g_f)]),
            scratch=(audio_scratch, bias_scratch, grad_scratch),
            est=cost(10 * HD * pairs, pairs, 5000000),
        )
        dk_own, dv_own, dk_far, dv_far, *back = call(
            lambda *refs: av_kernel(chips, *refs),
            "av",
            [smem] + [whole] * 16,
            [(whole, part)] * 4 + [(whole, piece)] * 6,
            (window, *pieces, k_v, v_v, k_f, v_f, stats_a, stats_b, by_a, by_b, by_q2, kv_grads),
            scratch=(audio_scratch, bias_scratch, grad_scratch, grad_scratch, audio_scratch),
            est=cost(12 * HD * pairs, pairs, 5000000),
        )
        parts = [back[0]] + [move(x, name) for x, name in zip(back[1:], ("aud", "A", "Ax", "B", "Bx"))]

        fars = [move(x, "core") for x in (out_far, dq_far, dk_far, dv_far)]
        out_video, dq_video, dk_video, dv_video, joined = call(
            join_video_kernel,
            "join_video",
            [whole] * 8,
            [(whole, full)] * 4 + [(whole, shape((8, PAIR), F32))],
            (out_own, dq_own, dk_own, dv_own, *fars),
            est=cost(0, 0, 1600000),
        )
        mine, other = call(
            sum_kernel, "sum_audio", [whole] * 8, [(whole, piece)] * 2, (mask, *parts, joined),
            est=cost(1000000, 0, 1600000),
        )
        other = move(other, "core")
        dk_audio, dv_audio, dq_audio, out_audio = call(
            join_audio_kernel,
            "join_audio",
            [whole] * 2,
            [(whole, shape((half, 2 * width), BF))] * 4,
            (mine, other),
            est=cost(0, 0, 800000),
        )
        return (out_video, out_audio, dq_video, dk_video, dv_video, dq_audio, dk_audio, dv_audio)

    return step


def solution(mesh):
    video, audio = P("vid", "aud"), P(("vid", "aud"), None)
    return jax.shard_map(
        make_body(mesh),
        mesh=mesh,
        in_specs=(video,) * 4 + (audio,) * 4 + (P(), P()),
        out_specs=(video, audio, video, video, video, audio, audio, audio),
        check_vma=False,
    )
```

profile of v0, /device:TPU:129, one launch (start us, length us, event | category | flops | bytes accessed | tf_op | source)
XLA Modules:
  0.0 81.2 jit_solution(16349978133555956747)
XLA Ops:
  0.6 0.8 collective-permute-start
  1.4 0.1 collective-permute-start.2
  1.5 0.4 collective-permute-start.3
  1.9 0.1 collective-permute-start.1
  2.0 0.4 collective-permute-start.11
  2.4 1.1 %load.1.mine = bf16[4,32,1536]{2,1,0:T(8,128)(2,1)S(1)} custom-call(bf16[32,1536]{1,0:T(8,128)(2,1)} %refs_0_.1, bf16[32,1536]{1,0:T(8,128)(2,1)} %refs_1_.1, bf16[32,1536]{1,0:T(8,128)(2,1)} %refs_2_.1, bf16[32,1536]{1,0:T(8,128)(2,1)} %refs_3_.2), custom_call_target="tpu_custom_call" | custom-call | bytes 800000 | tf_op jit(solution)/shard_map/load/pallas_call | solution.py:423
  3.6 0.0 copy-start.1
  3.6 0.0 copy-start
  3.6 0.0 collective-permute-done.2.refs_2_
  3.6 0.0 collective-permute-done.3.refs_3_
  3.7 0.6 pack.1
  4.3 0.0 copy-start.2
  4.3 2.6 %collective-permute-start.6 = (bf16[4,2,32,384]{3,2,1,0:T(8,128)(2,1)S(1)}, bf16[4,2,32,384]{3,2,1,0:T(8,128)(2,1)S(1)}, u32[]{:S(2)}, u32[]{:S(2)}) collective-permute-start(bf16[4,2,32,384]{3,2,1,0:T(8,128)(2,1)S(1)} %get-tuple-element.38), channel_id=1, source_target_pairs={{0,5},{1,4},{2,7},{3,6},{4,1},{5,0},{6,3},{7,2},{8,13},{9,12},{10,... | collective-permute-start | bytes 589832 | tf_op jit(solution)/shard_map/ppermute | solution.py:401
  6.8 0.5 collective-permute-start.4
  7.4 0.7 collective-permute-start.12
  8.0 0.3 collective-permute-start.5
  8.3 7.8 %collective-permute-done.6.refs_3_.refs_4_ = bf16[4,2,32,384]{3,2,1,0:T(8,128)(2,1)S(1)} collective-permute-done((bf16[4,2,32,384]{3,2,1,0:T(8,128)(2,1)S(1)}, bf16[4,2,32,384]{3,2,1,0:T(8,128)(2,1)S(1)}, u32[]{:S(2)}, u32[]{:S(2)}) %collective-permute-start.6) | collective-permute-done | bytes 196640 | tf_op jit(solution)/shard_map/ppermute | solution.py:401
  16.1 1.0 %collective-permute-start.9 = (bf16[256,768]{1,0:T(8,128)(2,1)S(1)}, bf16[256,768]{1,0:T(8,128)(2,1)S(1)}, u32[]{:S(2)}, u32[]{:S(2)}) collective-permute-start(bf16[256,768]{1,0:T(8,128)(2,1)S(1)} %copy-done.4), channel_id=1, source_target_pairs={{0,2},{1,3},{2,0},{3,1},{4,6},{5,7},{6,4},{7,5},{8,10},{9,11},{10,... | collective-permute-start | bytes 1179656 | tf_op jit(solution)/shard_map/ppermute | solution.py:401
  17.1 0.1 collective-permute-start.10
  17.2 0.0 collective-permute-done.5.refs_2_.refs_3_
  17.2 6.4 %collective-permute-start.8 = (bf16[4,2,32,384]{3,2,1,0:T(8,128)(2,1)S(1)}, bf16[4,2,32,384]{3,2,1,0:T(8,128)(2,1)S(1)}, u32[]{:S(2)}, u32[]{:S(2)}) collective-permute-start(bf16[4,2,32,384]{3,2,1,0:T(8,128)(2,1)S(1)} %get-tuple-element.38), channel_id=1, source_target_pairs={{4,9},{5,8},{6,11},{7,10},{8,5},{9,4},{10,7},{11,6},{12,17},{13,16... | collective-permute-start | bytes 589832 | tf_op jit(solution)/shard_map/ppermute | solution.py:401
  23.6 3.4 %collective-permute-start.7 = (bf16[4,2,32,384]{3,2,1,0:T(8,128)(2,1)S(1)}, bf16[4,2,32,384]{3,2,1,0:T(8,128)(2,1)S(1)}, u32[]{:S(2)}, u32[]{:S(2)}) collective-permute-start(bf16[4,2,32,384]{3,2,1,0:T(8,128)(2,1)S(1)} %get-tuple-element.37.refs_0_.refs_1_), channel_id=1, source_target_pairs={{4,8},{5,9},{6,10},{7,11},{8,4},{9,5},{10,6},{11,7},{12,16},{13,17... | collective-permute-start | bytes 589832 | tf_op jit(solution)/shard_map/ppermute | solution.py:401
  27.0 2.0 %stats_a.1.refs_7_.refs_11_ = f32[3,8,256]{2,1,0:T(8,128)S(1)} custom-call(s32[2,512]{1,0:T(2,128)S(1)} %bitcast.1, bf16[4,2,32,384]{3,2,1,0:T(8,128)(2,1)S(1)} %get-tuple-element.37.refs_0_.refs_1_, bf16[4,2,32,384]{3,2,1,0:T(8,128)(2,1)S(1)} %collective-permute-done.4.refs_1_.refs_2_, bf16[4,2,32,384]{3,2,1,0:T(8,128)(2,1)S(1)} %collective-permute-done.5.refs_2_.refs_3_, ...), custom_call_target="tpu_custom_call" | custom-call | flops 201326592 | bytes 2000000 | tf_op jit(solution)/shard_map/stats_a/pallas_call | solution.py:423
  29.0 0.1 collective-permute-start.13
  29.1 1.4 %collective-permute-done.8.refs_5_.refs_2_.refs_6_ = bf16[4,2,32,384]{3,2,1,0:T(8,128)(2,1)S(1)} collective-permute-done((bf16[4,2,32,384]{3,2,1,0:T(8,128)(2,1)S(1)}, bf16[4,2,32,384]{3,2,1,0:T(8,128)(2,1)S(1)}, u32[]{:S(2)}, u32[]{:S(2)}) %collective-permute-start.8) | collective-permute-done | bytes 196640 | tf_op jit(solution)/shard_map/ppermute | solution.py:401
  30.5 4.9 %collective-permute-done.7.refs_4_.refs_1_.refs_5_ = bf16[4,2,32,384]{3,2,1,0:T(8,128)(2,1)S(1)} collective-permute-done((bf16[4,2,32,384]{3,2,1,0:T(8,128)(2,1)S(1)}, bf16[4,2,32,384]{3,2,1,0:T(8,128)(2,1)S(1)}, u32[]{:S(2)}, u32[]{:S(2)}) %collective-permute-start.7) | collective-permute-done | bytes 196640 | tf_op jit(solution)/shard_map/ppermute | solution.py:401
  35.4 0.0 collective-permute-done.13.refs_8_.refs_13_
  35.4 1.5 %stats_b.1.refs_12_ = f32[3,8,256]{2,1,0:T(8,128)S(1)} custom-call(s32[2,512]{1,0:T(2,128)S(1)} %bitcast.2, bf16[4,2,32,384]{3,2,1,0:T(8,128)(2,1)S(1)} %collective-permute-done.7.refs_4_.refs_1_.refs_5_, bf16[4,2,32,384]{3,2,1,0:T(8,128)(2,1)S(1)} %collective-permute-done.8.refs_5_.refs_2_.refs_6_, bf16[256,768]{1,0:T(8,128)(2,1)S(1)} %copy-done, ...), custom_call_target="tpu_custom_call" | custom-call | flops 100663296 | bytes 2000000 | tf_op jit(solution)/shard_map/stats_b/pallas_call | solution.py:423
  36.9 1.9 %collective-permute-start.15 = (f32[3,8,256]{2,1,0:T(8,128)S(1)}, f32[3,8,256]{2,1,0:T(8,128)S(1)}, u32[]{:S(2)}, u32[]{:S(2)}) collective-permute-start(f32[3,8,256]{2,1,0:T(8,128)S(1)} %stats_b.1.refs_12_), channel_id=1, source_target_pairs={{4,12},{5,13},{6,14},{7,15},{8,0},{9,1},{10,2},{11,3},{12,20},{13,... | collective-permute-start | bytes 73736 | tf_op jit(solution)/shard_map/ppermute | solution.py:401
  38.9 4.3 %collective-permute-start.14 = (f32[3,8,256]{2,1,0:T(8,128)S(1)}, f32[3,8,256]{2,1,0:T(8,128)S(1)}, u32[]{:S(2)}, u32[]{:S(2)}) collective-permute-start(f32[3,8,256]{2,1,0:T(8,128)S(1)} %stats_b.1.refs_12_), channel_id=1, source_target_pairs={{4,8},{5,9},{6,10},{7,11},{8,4},{9,5},{10,6},{11,7},{12,16},{13,17... | collective-permute-start | bytes 73736 | tf_op jit(solution)/shard_map/ppermute | solution.py:401
  43.2 0.0 collective-permute-done.9.refs_8_
  43.2 4.2 %va.1 = (bf16[256,384]{1,0:T(8,128)(2,1)S(1)}, bf16[256,384]{1,0:T(8,128)(2,1)S(1)}, bf16[256,384]{1,0:T(8,128)(2,1)S(1)}, bf16[256,384]{1,0:T(8,128)(2,1)S(1)}, bf16[2,384,384]{2,1,0:T(8,128)(2,1)S(1)}) custom-call(s32[2,512]{1,0:T(2,128)S(1)} %bitcast.3, s32[128]{0:T(128)S(1)} %copy-done.3, bf16[4,2,32,384]{3,2,1,0:T(8,128)(2,1)S(1)} %get-tuple-element.37.refs_0_.refs_1_, ...), custom_call_target="tpu_custom_call" | custom-call | flops 754974720 | bytes 5000000 | tf_op jit(solution)/shard_map/va/pallas_call | solution.py:423
  47.4 4.0 %collective-permute-start.16 = (bf16[256,384]{1,0:T(8,128)(2,1)S(1)}, bf16[256,384]{1,0:T(8,128)(2,1)S(1)}, u32[]{:S(2)}, u32[]{:S(2)}) collective-permute-start(bf16[256,384]{1,0:T(8,128)(2,1)S(1)} %get-tuple-element.44), channel_id=1, source_target_pairs={{0,2},{1,3},{2,0},{3,1},{4,6},{5,7},{6,4},{7,5},{8,10},{9,11},{10,... | collective-permute-start | bytes 589832 | tf_op jit(solution)/shard_map/ppermute | solution.py:401
  51.5 0.3 collective-permute-start.17
  51.7 4.2 %av.1 = (bf16[256,384]{1,0:T(8,128)(2,1)S(1)}, bf16[256,384]{1,0:T(8,128)(2,1)S(1)}, bf16[256,384]{1,0:T(8,128)(2,1)S(1)}, bf16[256,384]{1,0:T(8,128)(2,1)S(1)},...) custom-call(s32[2,512]{1,0:T(2,128)S(1)} %bitcast.4, ...), custom_call_target="tpu_custom_call" | custom-call | flops 905969664 | bytes 5000000 | tf_op jit(solution)/shard_map/av/pallas_call | solution.py:423
  56.0 0.3 collective-permute-start.18
  56.3 0.3 collective-permute-start.19
  56.6 0.2 collective-permute-start.20
  56.8 3.0 %collective-permute-start.22 = (bf16[4,2,32,384]{3,2,1,0:T(8,128)(2,1)S(1)}, bf16[4,2,32,384]{3,2,1,0:T(8,128)(2,1)S(1)}, u32[]{:S(2)}, u32[]{:S(2)}) collective-permute-start(bf16[4,2,32,384]{3,2,1,0:T(8,128)(2,1)S(1)} %get-tuple-element.53), channel_id=1, source_target_pairs={{0,5},{1,4},{2,7},{3,6},{4,1},{5,0},{6,3},{7,2},{8,13},{9,12},{10,... | collective-permute-start | bytes 589832 | tf_op jit(solution)/shard_map/ppermute | solution.py:401
  59.8 4.6 %collective-permute-start.23 = (bf16[4,2,32,384]{3,2,1,0:T(8,128)(2,1)S(1)}, bf16[4,2,32,384]{3,2,1,0:T(8,128)(2,1)S(1)}, u32[]{:S(2)}, u32[]{:S(2)}) collective-permute-start(bf16[4,2,32,384]{3,2,1,0:T(8,128)(2,1)S(1)} %get-tuple-element.54), channel_id=1, source_target_pairs={{4,8},{5,9},{6,10},{7,11},{8,4},{9,5},{10,6},{11,7},{12,16},{13,17... | collective-permute-start | bytes 589832 | tf_op jit(solution)/shard_map/ppermute | solution.py:401
  64.5 3.9 %collective-permute-start.24 = (bf16[4,2,32,384]{3,2,1,0:T(8,128)(2,1)S(1)}, bf16[4,2,32,384]{3,2,1,0:T(8,128)(2,1)S(1)}, u32[]{:S(2)}, u32[]{:S(2)}) collective-permute-start(bf16[4,2,32,384]{3,2,1,0:T(8,128)(2,1)S(1)} %get-tuple-element.55), channel_id=1, source_target_pairs={{4,9},{5,8},{6,11},{7,10},{8,5},{9,4},{10,7},{11,6},{12,17},{13,16... | collective-permute-start | bytes 589832 | tf_op jit(solution)/shard_map/ppermute | solution.py:401
  68.4 1.3 %join_video.1 = (bf16[256,768]{1,0:T(8,128)(2,1)}, bf16[256,768]{1,0:T(8,128)(2,1)}, bf16[256,768]{1,0:T(8,128)(2,1)}, bf16[256,768]{1,0:T(8,128)(2,1)}, f32[8,128]{1,0:T(8,128)S(1)}) custom-call(bf16[256,384]{1,0:T(8,128)(2,1)S(1)} %get-tuple-element.39.refs_0_, bf16[256,384]{1,0:T(8,128)(2,1)S(1)} %get-tuple-element.40.refs_1_, ...), custom_call_target="tpu_custom_call" | custom-call | bytes 1600000 | tf_op jit(solution)/shard_map/join_video/pallas_call | solution.py:423
  69.7 1.6 %collective-permute-done.23.by_b = bf16[4,2,32,384]{3,2,1,0:T(8,128)(2,1)S(1)} collective-permute-done((bf16[4,2,32,384]{3,2,1,0:T(8,128)(2,1)S(1)}, bf16[4,2,32,384]{3,2,1,0:T(8,128)(2,1)S(1)}, u32[]{:S(2)}, u32[]{:S(2)}) %collective-permute-start.23) | collective-permute-done | bytes 196640 | tf_op jit(solution)/shard_map/ppermute | solution.py:401
  71.3 5.4 %collective-permute-done.24.by_bx = bf16[4,2,32,384]{3,2,1,0:T(8,128)(2,1)S(1)} collective-permute-done((bf16[4,2,32,384]{3,2,1,0:T(8,128)(2,1)S(1)}, bf16[4,2,32,384]{3,2,1,0:T(8,128)(2,1)S(1)}, u32[]{:S(2)}, u32[]{:S(2)}) %collective-permute-start.24) | collective-permute-done | bytes 196640 | tf_op jit(solution)/shard_map/ppermute | solution.py:401
  76.7 0.2 sum_audio.1
  76.9 2.5 %collective-permute-start.25 = (bf16[4,2,32,384]{3,2,1,0:T(8,128)(2,1)S(1)}, bf16[4,2,32,384]{3,2,1,0:T(8,128)(2,1)S(1)}, u32[]{:S(2)}, u32[]{:S(2)}) collective-permute-start(bf16[4,2,32,384]{3,2,1,0:T(8,128)(2,1)S(1)} %get-tuple-element.58), channel_id=1, source_target_pairs={{0,2},{1,3},{2,0},{3,1},{4,6},{5,7},{6,4},{7,5},{8,10},{9,11},{10,... | collective-permute-start | bytes 589832 | tf_op jit(solution)/shard_map/ppermute | solution.py:401
  79.4 1.1 %collective-permute-done.25.other = bf16[4,2,32,384]{3,2,1,0:T(8,128)(2,1)S(1)} collective-permute-done((bf16[4,2,32,384]{3,2,1,0:T(8,128)(2,1)S(1)}, bf16[4,2,32,384]{3,2,1,0:T(8,128)(2,1)S(1)}, u32[]{:S(2)}, u32[]{:S(2)}) %collective-permute-start.25) | collective-permute-done | bytes 196640 | tf_op jit(solution)/shard_map/ppermute | solution.py:401
  80.5 0.8 join_audio.1
  (25 shorter events, 0.1 us)
Async XLA Ops:
  0.6 3.0 %copy-start.3 = (s32[128]{0:T(128)S(1)}, s32[128]{0:T(128)}, u32[]{:S(2)}) copy-start(s32[128]{0:T(128)} %len_ref.3) | copy-start | bytes 1540
  0.6 3.0 %collective-permute-start = (bf16[32,1536]{1,0:T(8,128)(2,1)}, bf16[32,1536]{1,0:T(8,128)(2,1)S(1)}, u32[]{:S(2)}, u32[]{:S(2)}) collective-permute-start(bf16[32,1536]{1,0:T(8,128)(2,1)} %refs_0_.1), channel_id=1, source_target_pairs={{0,2},{1,3},{2,0},{3,1},{4,6},{5,7},{6,4},{7,5},{8,10},{9,11},{10,... | collective-permute-start | bytes 294920 | tf_op jit(solution)/shard_map/ppermute | solution.py:401
  1.4 2.2 %collective-permute-start.2 = (bf16[32,1536]{1,0:T(8,128)(2,1)}, bf16[32,1536]{1,0:T(8,128)(2,1)S(1)}, u32[]{:S(2)}, u32[]{:S(2)}) collective-permute-start(bf16[32,1536]{1,0:T(8,128)(2,1)} %refs_2_.1), channel_id=1, source_target_pairs={{0,2},{1,3},{2,0},{3,1},{4,6},{5,7},{6,4},{7,5},{8,10},{9,11},{10,... | collective-permute-start | bytes 294920 | tf_op jit(solution)/shard_map/ppermute | solution.py:401
  1.5 2.1 %collective-permute-start.3 = (bf16[32,1536]{1,0:T(8,128)(2,1)}, bf16[32,1536]{1,0:T(8,128)(2,1)S(1)}, u32[]{:S(2)}, u32[]{:S(2)}) collective-permute-start(bf16[32,1536]{1,0:T(8,128)(2,1)} %refs_3_.2), channel_id=1, source_target_pairs={{0,2},{1,3},{2,0},{3,1},{4,6},{5,7},{6,4},{7,5},{8,10},{9,11},{10,... | collective-permute-start | bytes 294920 | tf_op jit(solution)/shard_map/ppermute | solution.py:401
  1.9 1.7 %collective-permute-start.1 = (bf16[32,1536]{1,0:T(8,128)(2,1)}, bf16[32,1536]{1,0:T(8,128)(2,1)S(1)}, u32[]{:S(2)}, u32[]{:S(2)}) collective-permute-start(bf16[32,1536]{1,0:T(8,128)(2,1)} %refs_1_.1), channel_id=1, source_target_pairs={{0,2},{1,3},{2,0},{3,1},{4,6},{5,7},{6,4},{7,5},{8,10},{9,11},{10,... | collective-permute-start | bytes 294920 | tf_op jit(solution)/shard_map/ppermute | solution.py:401
  2.0 21.6 %collective-permute-start.11 = (bf16[256,768]{1,0:T(8,128)(2,1)}, bf16[256,768]{1,0:T(8,128)(2,1)S(1)}, u32[]{:S(2)}, u32[]{:S(2)}) collective-permute-start(bf16[256,768]{1,0:T(8,128)(2,1)} %refs_7_.3), channel_id=1, source_target_pairs={{0,2},{1,3},{2,0},{3,1},{4,6},{5,7},{6,4},{7,5},{8,10},{9,11},{10,... | collective-permute-start | bytes 1179656 | tf_op jit(solution)/shard_map/ppermute | solution.py:401
  2.4 13.7 %copy-start.4 = (bf16[256,768]{1,0:T(8,128)(2,1)S(1)}, bf16[256,768]{1,0:T(8,128)(2,1)}, u32[]{:S(2)}) copy-start(bf16[256,768]{1,0:T(8,128)(2,1)} %refs_6_.2) | copy-start | bytes 1179652
  2.4 14.7 %copy-start.5 = (bf16[256,768]{1,0:T(8,128)(2,1)S(1)}, bf16[256,768]{1,0:T(8,128)(2,1)}, u32[]{:S(2)}) copy-start(bf16[256,768]{1,0:T(8,128)(2,1)} %refs_7_.2) | copy-start | bytes 1179652
  3.6 3.8 %copy-start.1 = (bf16[256,768]{1,0:T(8,128)(2,1)S(1)}, bf16[256,768]{1,0:T(8,128)(2,1)}, u32[]{:S(2)}) copy-start(bf16[256,768]{1,0:T(8,128)(2,1)} %refs_8_.1) | copy-start | bytes 1179652
  3.6 23.4 %copy-start = (bf16[256,768]{1,0:T(8,128)(2,1)S(1)}, bf16[256,768]{1,0:T(8,128)(2,1)}, u32[]{:S(2)}) copy-start(bf16[256,768]{1,0:T(8,128)(2,1)} %refs_7_.3) | copy-start | bytes 1179652
  4.3 22.7 %copy-start.2 = (s32[512,2]{0,1:T(2,128)S(1)}, s32[512,2]{0,1:T(2,128)}, u32[]{:S(2)}) copy-start(s32[512,2]{0,1:T(2,128)} %param.18) | copy-start | bytes 12292
  4.3 11.9 %collective-permute-start.6 = (bf16[4,2,32,384]{3,2,1,0:T(8,128)(2,1)S(1)}, bf16[4,2,32,384]{3,2,1,0:T(8,128)(2,1)S(1)}, u32[]{:S(2)}, u32[]{:S(2)}) collective-permute-start(bf16[4,2,32,384]{3,2,1,0:T(8,128)(2,1)S(1)} %get-tuple-element.38), channel_id=1, source_target_pairs={{0,5},{1,4},{2,7},{3,6},{4,1},{5,0},{6,3},{7,2},{8,13},{9,12},{10,... | collective-permute-start | bytes 589832 | tf_op jit(solution)/shard_map/ppermute | solution.py:401
  6.8 10.3 %collective-permute-start.4 = (bf16[4,2,32,384]{3,2,1,0:T(8,128)(2,1)S(1)}, bf16[4,2,32,384]{3,2,1,0:T(8,128)(2,1)S(1)}, u32[]{:S(2)}, u32[]{:S(2)}) collective-permute-start(bf16[4,2,32,384]{3,2,1,0:T(8,128)(2,1)S(1)} %get-tuple-element.38), channel_id=1, source_target_pairs={{0,1},{1,0},{2,3},{3,2},{4,5},{5,4},{6,7},{7,6},{8,9},{9,8},{10,11... | collective-permute-start | bytes 589832 | tf_op jit(solution)/shard_map/ppermute | solution.py:401
  7.4 19.6 %collective-permute-start.12 = (bf16[256,768]{1,0:T(8,128)(2,1)S(1)}, bf16[256,768]{1,0:T(8,128)(2,1)S(1)}, u32[]{:S(2)}, u32[]{:S(2)}) collective-permute-start(bf16[256,768]{1,0:T(8,128)(2,1)S(1)} %copy-done.1), channel_id=1, source_target_pairs={{0,2},{1,3},{2,0},{3,1},{4,6},{5,7},{6,4},{7,5},{8,10},{9,11},{10,... | collective-permute-start | bytes 1179656 | tf_op jit(solution)/shard_map/ppermute | solution.py:401
  8.0 9.2 %collective-permute-start.5 = (bf16[4,2,32,384]{3,2,1,0:T(8,128)(2,1)S(1)}, bf16[4,2,32,384]{3,2,1,0:T(8,128)(2,1)S(1)}, u32[]{:S(2)}, u32[]{:S(2)}) collective-permute-start(bf16[4,2,32,384]{3,2,1,0:T(8,128)(2,1)S(1)} %get-tuple-element.37.refs_0_.refs_1_), channel_id=1, source_target_pairs={{0,4},{1,5},{2,6},{3,7},{4,0},{5,1},{6,2},{7,3},{8,12},{9,13},{10,... | collective-permute-start | bytes 589832 | tf_op jit(solution)/shard_map/ppermute | solution.py:401
  16.1 27.0 %collective-permute-start.9 = (bf16[256,768]{1,0:T(8,128)(2,1)S(1)}, bf16[256,768]{1,0:T(8,128)(2,1)S(1)}, u32[]{:S(2)}, u32[]{:S(2)}) collective-permute-start(bf16[256,768]{1,0:T(8,128)(2,1)S(1)} %copy-done.4), channel_id=1, source_target_pairs={{0,2},{1,3},{2,0},{3,1},{4,6},{5,7},{6,4},{7,5},{8,10},{9,11},{10,... | collective-permute-start | bytes 1179656 | tf_op jit(solution)/shard_map/ppermute | solution.py:401
  17.1 26.1 %collective-permute-start.10 = (bf16[256,768]{1,0:T(8,128)(2,1)S(1)}, bf16[256,768]{1,0:T(8,128)(2,1)S(1)}, u32[]{:S(2)}, u32[]{:S(2)}) collective-permute-start(bf16[256,768]{1,0:T(8,128)(2,1)S(1)} %copy-done.5), channel_id=1, source_target_pairs={{0,2},{1,3},{2,0},{3,1},{4,6},{5,7},{6,4},{7,5},{8,10},{9,11},{10,... | collective-permute-start | bytes 1179656 | tf_op jit(solution)/shard_map/ppermute | solution.py:401
  17.2 13.3 %collective-permute-start.8 = (bf16[4,2,32,384]{3,2,1,0:T(8,128)(2,1)S(1)}, bf16[4,2,32,384]{3,2,1,0:T(8,128)(2,1)S(1)}, u32[]{:S(2)}, u32[]{:S(2)}) collective-permute-start(bf16[4,2,32,384]{3,2,1,0:T(8,128)(2,1)S(1)} %get-tuple-element.38), channel_id=1, source_target_pairs={{4,9},{5,8},{6,11},{7,10},{8,5},{9,4},{10,7},{11,6},{12,17},{13,16... | collective-permute-start | bytes 589832 | tf_op jit(solution)/shard_map/ppermute | solution.py:401
  23.6 11.8 %collective-permute-start.7 = (bf16[4,2,32,384]{3,2,1,0:T(8,128)(2,1)S(1)}, bf16[4,2,32,384]{3,2,1,0:T(8,128)(2,1)S(1)}, u32[]{:S(2)}, u32[]{:S(2)}) collective-permute-start(bf16[4,2,32,384]{3,2,1,0:T(8,128)(2,1)S(1)} %get-tuple-element.37.refs_0_.refs_1_), channel_id=1, source_target_pairs={{4,8},{5,9},{6,10},{7,11},{8,4},{9,5},{10,6},{11,7},{12,16},{13,17... | collective-permute-start | bytes 589832 | tf_op jit(solution)/shard_map/ppermute | solution.py:401
  29.0 6.4 %collective-permute-start.13 = (f32[3,8,256]{2,1,0:T(8,128)S(1)}, f32[3,8,256]{2,1,0:T(8,128)S(1)}, u32[]{:S(2)}, u32[]{:S(2)}) collective-permute-start(f32[3,8,256]{2,1,0:T(8,128)S(1)} %stats_a.1.refs_7_.refs_11_), channel_id=1, source_target_pairs={{0,4},{1,5},{2,6},{3,7},{4,0},{5,1},{6,2},{7,3},{8,12},{9,13},{10,... | collective-permute-start | bytes 73736 | tf_op jit(solution)/shard_map/ppermute | solution.py:401
  36.9 14.8 %collective-permute-start.15 = (f32[3,8,256]{2,1,0:T(8,128)S(1)}, f32[3,8,256]{2,1,0:T(8,128)S(1)}, u32[]{:S(2)}, u32[]{:S(2)}) collective-permute-start(f32[3,8,256]{2,1,0:T(8,128)S(1)} %stats_b.1.refs_12_), channel_id=1, source_target_pairs={{4,12},{5,13},{6,14},{7,15},{8,0},{9,1},{10,2},{11,3},{12,20},{13,... | collective-permute-start | bytes 73736 | tf_op jit(solution)/shard_map/ppermute | solution.py:401
  38.9 12.9 %collective-permute-start.14 = (f32[3,8,256]{2,1,0:T(8,128)S(1)}, f32[3,8,256]{2,1,0:T(8,128)S(1)}, u32[]{:S(2)}, u32[]{:S(2)}) collective-permute-start(f32[3,8,256]{2,1,0:T(8,128)S(1)} %stats_b.1.refs_12_), channel_id=1, source_target_pairs={{4,8},{5,9},{6,10},{7,11},{8,4},{9,5},{10,6},{11,7},{12,16},{13,17... | collective-permute-start | bytes 73736 | tf_op jit(solution)/shard_map/ppermute | solution.py:401
  47.4 9.4 %collective-permute-start.16 = (bf16[256,384]{1,0:T(8,128)(2,1)S(1)}, bf16[256,384]{1,0:T(8,128)(2,1)S(1)}, u32[]{:S(2)}, u32[]{:S(2)}) collective-permute-start(bf16[256,384]{1,0:T(8,128)(2,1)S(1)} %get-tuple-element.44), channel_id=1, source_target_pairs={{0,2},{1,3},{2,0},{3,1},{4,6},{5,7},{6,4},{7,5},{8,10},{9,11},{10,... | collective-permute-start | bytes 589832 | tf_op jit(solution)/shard_map/ppermute | solution.py:401
  51.5 5.4 %collective-permute-start.17 = (bf16[256,384]{1,0:T(8,128)(2,1)S(1)}, bf16[256,384]{1,0:T(8,128)(2,1)S(1)}, u32[]{:S(2)}, u32[]{:S(2)}) collective-permute-start(bf16[256,384]{1,0:T(8,128)(2,1)S(1)} %get-tuple-element.45), channel_id=1, source_target_pairs={{0,2},{1,3},{2,0},{3,1},{4,6},{5,7},{6,4},{7,5},{8,10},{9,11},{10,... | collective-permute-start | bytes 589832 | tf_op jit(solution)/shard_map/ppermute | solution.py:401
  56.0 3.9 %collective-permute-start.18 = (bf16[256,384]{1,0:T(8,128)(2,1)S(1)}, bf16[256,384]{1,0:T(8,128)(2,1)S(1)}, u32[]{:S(2)}, u32[]{:S(2)}) collective-permute-start(bf16[256,384]{1,0:T(8,128)(2,1)S(1)} %get-tuple-element.46), channel_id=1, source_target_pairs={{0,2},{1,3},{2,0},{3,1},{4,6},{5,7},{6,4},{7,5},{8,10},{9,11},{10,... | collective-permute-start | bytes 589832 | tf_op jit(solution)/shard_map/ppermute | solution.py:401
  56.3 8.2 %collective-permute-start.19 = (bf16[256,384]{1,0:T(8,128)(2,1)S(1)}, bf16[256,384]{1,0:T(8,128)(2,1)S(1)}, u32[]{:S(2)}, u32[]{:S(2)}) collective-permute-start(bf16[256,384]{1,0:T(8,128)(2,1)S(1)} %get-tuple-element.47), channel_id=1, source_target_pairs={{0,2},{1,3},{2,0},{3,1},{4,6},{5,7},{6,4},{7,5},{8,10},{9,11},{10,... | collective-permute-start | bytes 589832 | tf_op jit(solution)/shard_map/ppermute | solution.py:401
  56.6 13.1 %collective-permute-start.20 = (bf16[4,2,32,384]{3,2,1,0:T(8,128)(2,1)S(1)}, bf16[4,2,32,384]{3,2,1,0:T(8,128)(2,1)S(1)}, u32[]{:S(2)}, u32[]{:S(2)}) collective-permute-start(bf16[4,2,32,384]{3,2,1,0:T(8,128)(2,1)S(1)} %get-tuple-element.51), channel_id=1, source_target_pairs={{0,1},{1,0},{2,3},{3,2},{4,5},{5,4},{6,7},{7,6},{8,9},{9,8},{10,11... | collective-permute-start | bytes 589832 | tf_op jit(solution)/shard_map/ppermute | solution.py:401
  56.8 12.9 %collective-permute-start.21 = (bf16[4,2,32,384]{3,2,1,0:T(8,128)(2,1)S(1)}, bf16[4,2,32,384]{3,2,1,0:T(8,128)(2,1)S(1)}, u32[]{:S(2)}, u32[]{:S(2)}) collective-permute-start(bf16[4,2,32,384]{3,2,1,0:T(8,128)(2,1)S(1)} %get-tuple-element.52), channel_id=1, source_target_pairs={{0,4},{1,5},{2,6},{3,7},{4,0},{5,1},{6,2},{7,3},{8,12},{9,13},{10,... | collective-permute-start | bytes 589832 | tf_op jit(solution)/shard_map/ppermute | solution.py:401
  56.8 12.9 %collective-permute-start.22 = (bf16[4,2,32,384]{3,2,1,0:T(8,128)(2,1)S(1)}, bf16[4,2,32,384]{3,2,1,0:T(8,128)(2,1)S(1)}, u32[]{:S(2)}, u32[]{:S(2)}) collective-permute-start(bf16[4,2,32,384]{3,2,1,0:T(8,128)(2,1)S(1)} %get-tuple-element.53), channel_id=1, source_target_pairs={{0,5},{1,4},{2,7},{3,6},{4,1},{5,0},{6,3},{7,2},{8,13},{9,12},{10,... | collective-permute-start | bytes 589832 | tf_op jit(solution)/shard_map/ppermute | solution.py:401
  59.8 11.5 %collective-permute-start.23 = (bf16[4,2,32,384]{3,2,1,0:T(8,128)(2,1)S(1)}, bf16[4,2,32,384]{3,2,1,0:T(8,128)(2,1)S(1)}, u32[]{:S(2)}, u32[]{:S(2)}) collective-permute-start(bf16[4,2,32,384]{3,2,1,0:T(8,128)(2,1)S(1)} %get-tuple-element.54), channel_id=1, source_target_pairs={{4,8},{5,9},{6,10},{7,11},{8,4},{9,5},{10,6},{11,7},{12,16},{13,17... | collective-permute-start | bytes 589832 | tf_op jit(solution)/shard_map/ppermute | solution.py:401
  64.5 12.3 %collective-permute-start.24 = (bf16[4,2,32,384]{3,2,1,0:T(8,128)(2,1)S(1)}, bf16[4,2,32,384]{3,2,1,0:T(8,128)(2,1)S(1)}, u32[]{:S(2)}, u32[]{:S(2)}) collective-permute-start(bf16[4,2,32,384]{3,2,1,0:T(8,128)(2,1)S(1)} %get-tuple-element.55), channel_id=1, source_target_pairs={{4,9},{5,8},{6,11},{7,10},{8,5},{9,4},{10,7},{11,6},{12,17},{13,16... | collective-permute-start | bytes 589832 | tf_op jit(solution)/shard_map/ppermute | solution.py:401
  76.9 3.5 %collective-permute-start.25 = (bf16[4,2,32,384]{3,2,1,0:T(8,128)(2,1)S(1)}, bf16[4,2,32,384]{3,2,1,0:T(8,128)(2,1)S(1)}, u32[]{:S(2)}, u32[]{:S(2)}) collective-permute-start(bf16[4,2,32,384]{3,2,1,0:T(8,128)(2,1)S(1)} %get-tuple-element.58), channel_id=1, source_target_pairs={{0,2},{1,3},{2,0},{3,1},{4,6},{5,7},{6,4},{7,5},{8,10},{9,11},{10,... | collective-permute-start | bytes 589832 | tf_op jit(solution)/shard_map/ppermute | solution.py:401
where the time goes:
time: 81.5 us; the launch traced here: 81.2 us
  starting transfers between devices  42.1 us (52%)
  waiting for transfers between devices  22.3 us (27%)
  Pallas kernels  16 us (20%)
  between operations  0.89 us (1%)
    ppermute x26, starting transfers between devices, move(): return lax.ppermute(x, ('vid', 'aud'), moves[name])  42.1 us
    ppermute x26, waiting for transfers between devices, move(): return lax.ppermute(x, ('vid', 'aud'), moves[name])  22.3 us
    pallas_call x9, Pallas kernels, call(): pl.pallas_call(kernel, in_specs=ins, out_specs=outs, scratch_shapes=list(...  16 us
  transfers between devices with their start and end apart: 26, of which 6 were waited for; matrix products, arithmetic and copies ran while one was open for 0% of the time, Pallas kernels for 18%

commit v1 on v0

--- a/solution.py
+++ b/solution.py
@@ -246,8 +246,8 @@
 def va_kernel(win_ref, len_ref, *refs):
     pieces = refs[:6]
     video = ((refs[6], refs[7]), (refs[8], refs[9]))
-    outs = ((refs[10], refs[11]), (refs[12], refs[13]))
-    kv_grads, audio, bias, grads = refs[14:]
+    outs = ((refs[10], refs[11]), (refs[12].at[0], refs[12].at[1]))
+    kv_grads, audio, bias, grads = refs[13:]
     _, r, _ = coords()
     quarter = audio.shape[2]
     block_bias(win_ref, len_ref, bias)
@@ -292,9 +292,9 @@
     pieces = refs[:6]
     video = ((refs[6], refs[7]), (refs[8], refs[9]))
     stats, kv_grads = refs[10:15], refs[15]
-    outs = ((refs[16], refs[17]), (refs[18], refs[19]))
-    back = refs[20:26]
-    audio, bias, grads, rowstat, qo_grads = refs[26:]
+    outs = ((refs[16], refs[17]), (refs[18].at[0], refs[18].at[1]))
+    back = refs[19:25]
+    audio, bias, grads, rowstat, qo_grads = refs[25:]
     c, r, _ = coords()
     quarter = audio.shape[2]
     block_bias(win_ref, None, bias)
@@ -361,10 +361,11 @@
 def join_video_kernel(*refs):
     _, r, _ = coords()
     quarter = refs[0].shape[1]
-    for own, far, out in zip(refs[:4], refs[4:8], refs[8:12]):
+    fars = [ref.at[n] for ref in refs[4:6] for n in range(2)]
+    for own, far, out in zip(refs[:4], fars, refs[6:10]):
         for core, src in ((r, own), (1 - r, far)):
             out[:, pl.ds(pl.multiple_of(core * quarter, PAIR), quarter)] = src[...]
-    refs[12][...] = jnp.zeros(refs[12].shape, F32)
+    refs[10][...] = jnp.zeros(refs[10].shape, F32)
 
 
 def cost(flops, transcendentals, nbytes):
@@ -472,32 +473,33 @@
         stats_b = find_stats((2,), "stats_b", (stats_a, by_a))
         by_b, by_q2 = move(stats_b, "B"), move(stats_b, "Q2")
 
+        far = shape((2, rows, quarter), BF)
         full, part = shape((rows, width), BF), shape((rows, quarter), BF)
-        out_own, dq_own, out_far, dq_far, kv_grads = call(
+        out_own, dq_own, va_far, kv_grads = call(
             va_kernel,
             "va",
             [smem, smem] + [whole] * 10,
-            [(whole, part)] * 4 + [(whole, shape((2, KEYS, quarter), BF))],
+            [(whole, part)] * 2 + [(whole, far)] + [(whole, shape((2, KEYS, quarter), BF))],
             (window, audio_len, *pieces, *[pltpu.with_memory_space_constraint(x, pltpu.VMEM) for x in (q_v, g_v, q_f, g_f)]),
             scratch=(audio_scratch, bias_scratch, grad_scratch),
             est=cost(10 * HD * pairs, pairs, 5000000),
         )
-        dk_own, dv_own, dk_far, dv_far, *back = call(
+        dk_own, dv_own, av_far, *back = call(
             lambda *refs: av_kernel(chips, *refs),
             "av",
             [smem] + [whole] * 16,
-            [(whole, part)] * 4 + [(whole, piece)] * 6,
+            [(whole, part)] * 2 + [(whole, far)] + [(whole, piece)] * 6,
             (window, *pieces, k_v, v_v, k_f, v_f, stats_a, stats_b, by_a, by_b, by_q2, kv_grads),
             scratch=(audio_scratch, bias_scratch, grad_scratch, grad_scratch, audio_scratch),
             est=cost(12 * HD * pairs, pairs, 5000000),
         )
         parts = [back[0]] + [move(x, name) for x, name in zip(back[1:], ("aud", "A", "Ax", "B", "Bx"))]
 
-        fars = [move(x, "core") for x in (out_far, dq_far, dk_far, dv_far)]
+        fars = [move(x, "core") for x in (va_far, av_far)]
         out_video, dq_video, dk_video, dv_video, joined = call(
             join_video_kernel,
             "join_video",
-            [whole] * 8,
+            [whole] * 6,
             [(whole, full)] * 4 + [(whole, shape((8, PAIR), F32))],
             (out_own, dq_own, dk_own, dv_own, *fars),
             est=cost(0, 0, 1600000),

time: 81.5 us -> 81.4 us (level)
    ppermute x26 -> x24, starting transfers between devices: 42.1 us -> 41.3 us  [move(): return lax.ppermute(x, ('vid', 'aud'), moves[name])]
    ppermute x26 -> x24, waiting for transfers between devices: 22.3 us -> 23 us  [move(): return lax.ppermute(x, ('vid', 'aud'), moves[name])]
  transfers between devices with their start and end apart: 26 -> 24, of which waited for: 6 -> 6; matrix products, arithmetic and copies ran while one was open for 0% -> 0% of each run, Pallas kernels for 18% -> 18%
where the time goes in v1:
time: 81.4 us; the launch traced here: 81.1 us
  starting transfers between devices  41.3 us (51%)
  waiting for transfers between devices  23 us (28%)
  Pallas kernels  15.9 us (20%)
  between operations  0.89 us (1%)
    ppermute x24, starting transfers between devices, move(): return lax.ppermute(x, ('vid', 'aud'), moves[name])  41.3 us
    ppermute x24, waiting for transfers between devices, move(): return lax.ppermute(x, ('vid', 'aud'), moves[name])  23 us
    pallas_call x9, Pallas kernels, call(): pl.pallas_call(kernel, in_specs=ins, out_specs=outs, scratch_shapes=list(...  15.9 us
  transfers between devices with their start and end apart: 24, of which 6 were waited for; matrix products, arithmetic and copies ran while one was open for 0% of the time, Pallas kernels for 18%

profile of v1, /device:TPU:129, one launch (start us, length us, event | category | flops | bytes accessed | tf_op | source)
XLA Modules:
  0.0 81.1 jit_solution(8479175779555320590)
XLA Ops:
  0.6 0.8 collective-permute-start
  1.4 0.1 collective-permute-start.2
  1.5 0.4 collective-permute-start.3
  1.9 0.1 collective-permute-start.1
  2.0 0.4 collective-permute-start.11
  2.4 1.1 %load.1.mine = bf16[4,32,1536]{2,1,0:T(8,128)(2,1)S(1)} custom-call(bf16[32,1536]{1,0:T(8,128)(2,1)} %refs_0_.1, bf16[32,1536]{1,0:T(8,128)(2,1)} %refs_1_.1, bf16[32,1536]{1,0:T(8,128)(2,1)} %refs_2_.1, bf16[32,1536]{1,0:T(8,128)(2,1)} %refs_3_.2), custom_call_target="tpu_custom_call" | custom-call | bytes 800000 | tf_op jit(solution)/shard_map/load/pallas_call | solution.py:424
  3.6 0.0 copy-start.1
  3.6 0.0 copy-start
  3.6 0.0 collective-permute-done.2.refs_2_
  3.6 0.0 collective-permute-done.3.refs_3_
  3.7 0.6 pack.1
  4.3 0.0 copy-start.2
  4.3 2.6 %collective-permute-start.6 = (bf16[4,2,32,384]{3,2,1,0:T(8,128)(2,1)S(1)}, bf16[4,2,32,384]{3,2,1,0:T(8,128)(2,1)S(1)}, u32[]{:S(2)}, u32[]{:S(2)}) collective-permute-start(bf16[4,2,32,384]{3,2,1,0:T(8,128)(2,1)S(1)} %get-tuple-element.36), channel_id=1, source_target_pairs={{0,5},{1,4},{2,7},{3,6},{4,1},{5,0},{6,3},{7,2},{8,13},{9,12},{10,... | collective-permute-start | bytes 589832 | tf_op jit(solution)/shard_map/ppermute | solution.py:402
  6.8 0.5 collective-permute-start.4
  7.4 0.7 collective-permute-start.12
  8.0 0.3 collective-permute-start.5
  8.3 7.8 %collective-permute-done.6.refs_3_.refs_4_ = bf16[4,2,32,384]{3,2,1,0:T(8,128)(2,1)S(1)} collective-permute-done((bf16[4,2,32,384]{3,2,1,0:T(8,128)(2,1)S(1)}, bf16[4,2,32,384]{3,2,1,0:T(8,128)(2,1)S(1)}, u32[]{:S(2)}, u32[]{:S(2)}) %collective-permute-start.6) | collective-permute-done | bytes 196640 | tf_op jit(solution)/shard_map/ppermute | solution.py:402
  16.1 1.0 %collective-permute-start.9 = (bf16[256,768]{1,0:T(8,128)(2,1)S(1)}, bf16[256,768]{1,0:T(8,128)(2,1)S(1)}, u32[]{:S(2)}, u32[]{:S(2)}) collective-permute-start(bf16[256,768]{1,0:T(8,128)(2,1)S(1)} %copy-done.4), channel_id=1, source_target_pairs={{0,2},{1,3},{2,0},{3,1},{4,6},{5,7},{6,4},{7,5},{8,10},{9,11},{10,... | collective-permute-start | bytes 1179656 | tf_op jit(solution)/shard_map/ppermute | solution.py:402
  17.1 0.1 collective-permute-start.10
  17.2 0.0 collective-permute-done.5.refs_2_.refs_3_
  17.2 6.4 %collective-permute-start.8 = (bf16[4,2,32,384]{3,2,1,0:T(8,128)(2,1)S(1)}, bf16[4,2,32,384]{3,2,1,0:T(8,128)(2,1)S(1)}, u32[]{:S(2)}, u32[]{:S(2)}) collective-permute-start(bf16[4,2,32,384]{3,2,1,0:T(8,128)(2,1)S(1)} %get-tuple-element.36), channel_id=1, source_target_pairs={{4,9},{5,8},{6,11},{7,10},{8,5},{9,4},{10,7},{11,6},{12,17},{13,16... | collective-permute-start | bytes 589832 | tf_op jit(solution)/shard_map/ppermute | solution.py:402
  23.6 3.4 %collective-permute-start.7 = (bf16[4,2,32,384]{3,2,1,0:T(8,128)(2,1)S(1)}, bf16[4,2,32,384]{3,2,1,0:T(8,128)(2,1)S(1)}, u32[]{:S(2)}, u32[]{:S(2)}) collective-permute-start(bf16[4,2,32,384]{3,2,1,0:T(8,128)(2,1)S(1)} %get-tuple-element.35.refs_0_.refs_1_), channel_id=1, source_target_pairs={{4,8},{5,9},{6,10},{7,11},{8,4},{9,5},{10,6},{11,7},{12,16},{13,17... | collective-permute-start | bytes 589832 | tf_op jit(solution)/shard_map/ppermute | solution.py:402
  27.0 2.0 %stats_a.1.refs_7_.refs_11_ = f32[3,8,256]{2,1,0:T(8,128)S(1)} custom-call(s32[2,512]{1,0:T(2,128)S(1)} %bitcast.1, bf16[4,2,32,384]{3,2,1,0:T(8,128)(2,1)S(1)} %get-tuple-element.35.refs_0_.refs_1_, bf16[4,2,32,384]{3,2,1,0:T(8,128)(2,1)S(1)} %collective-permute-done.4.refs_1_.refs_2_, bf16[4,2,32,384]{3,2,1,0:T(8,128)(2,1)S(1)} %collective-permute-done.5.refs_2_.refs_3_, ...), custom_call_target="tpu_custom_call" | custom-call | flops 201326592 | bytes 2000000 | tf_op jit(solution)/shard_map/stats_a/pallas_call | solution.py:424
  29.0 0.1 collective-permute-start.13
  29.1 1.4 %collective-permute-done.8.refs_5_.refs_2_.refs_6_ = bf16[4,2,32,384]{3,2,1,0:T(8,128)(2,1)S(1)} collective-permute-done((bf16[4,2,32,384]{3,2,1,0:T(8,128)(2,1)S(1)}, bf16[4,2,32,384]{3,2,1,0:T(8,128)(2,1)S(1)}, u32[]{:S(2)}, u32[]{:S(2)}) %collective-permute-start.8) | collective-permute-done | bytes 196640 | tf_op jit(solution)/shard_map/ppermute | solution.py:402
  30.5 4.9 %collective-permute-done.7.refs_4_.refs_1_.refs_5_ = bf16[4,2,32,384]{3,2,1,0:T(8,128)(2,1)S(1)} collective-permute-done((bf16[4,2,32,384]{3,2,1,0:T(8,128)(2,1)S(1)}, bf16[4,2,32,384]{3,2,1,0:T(8,128)(2,1)S(1)}, u32[]{:S(2)}, u32[]{:S(2)}) %collective-permute-start.7) | collective-permute-done | bytes 196640 | tf_op jit(solution)/shard_map/ppermute | solution.py:402
  35.4 0.0 collective-permute-done.13.refs_8_.refs_13_
  35.4 1.5 %stats_b.1.refs_12_ = f32[3,8,256]{2,1,0:T(8,128)S(1)} custom-call(s32[2,512]{1,0:T(2,128)S(1)} %bitcast.2, bf16[4,2,32,384]{3,2,1,0:T(8,128)(2,1)S(1)} %collective-permute-done.7.refs_4_.refs_1_.refs_5_, bf16[4,2,32,384]{3,2,1,0:T(8,128)(2,1)S(1)} %collective-permute-done.8.refs_5_.refs_2_.refs_6_, bf16[256,768]{1,0:T(8,128)(2,1)S(1)} %copy-done, ...), custom_call_target="tpu_custom_call" | custom-call | flops 100663296 | bytes 2000000 | tf_op jit(solution)/shard_map/stats_b/pallas_call | solution.py:424
  36.9 1.9 %collective-permute-start.15 = (f32[3,8,256]{2,1,0:T(8,128)S(1)}, f32[3,8,256]{2,1,0:T(8,128)S(1)}, u32[]{:S(2)}, u32[]{:S(2)}) collective-permute-start(f32[3,8,256]{2,1,0:T(8,128)S(1)} %stats_b.1.refs_12_), channel_id=1, source_target_pairs={{4,12},{5,13},{6,14},{7,15},{8,0},{9,1},{10,2},{11,3},{12,20},{13,... | collective-permute-start | bytes 73736 | tf_op jit(solution)/shard_map/ppermute | solution.py:402
  38.9 4.3 %collective-permute-start.14 = (f32[3,8,256]{2,1,0:T(8,128)S(1)}, f32[3,8,256]{2,1,0:T(8,128)S(1)}, u32[]{:S(2)}, u32[]{:S(2)}) collective-permute-start(f32[3,8,256]{2,1,0:T(8,128)S(1)} %stats_b.1.refs_12_), channel_id=1, source_target_pairs={{4,8},{5,9},{6,10},{7,11},{8,4},{9,5},{10,6},{11,7},{12,16},{13,17... | collective-permute-start | bytes 73736 | tf_op jit(solution)/shard_map/ppermute | solution.py:402
  43.2 0.0 collective-permute-done.9.refs_8_
  43.2 4.2 %va.1 = (bf16[256,384]{1,0:T(8,128)(2,1)S(1)}, bf16[256,384]{1,0:T(8,128)(2,1)S(1)}, bf16[2,256,384]{2,1,0:T(8,128)(2,1)S(1)}, bf16[2,384,384]{2,1,0:T(8,128)(2,1)S(1)}) custom-call(s32[2,512]{1,0:T(2,128)S(1)} %bitcast.3, s32[128]{0:T(128)S(1)} %copy-done.3, bf16[4,2,32,384]{3,2,1,0:T(8,128)(2,1)S(1)} %get-tuple-element.35.refs_0_.refs_1_, ...), custom_call_target="tpu_custom_call" | custom-call | flops 754974720 | bytes 5000000 | tf_op jit(solution)/shard_map/va/pallas_call | solution.py:424
  47.4 4.2 %collective-permute-start.16 = (bf16[2,256,384]{2,1,0:T(8,128)(2,1)S(1)}, bf16[2,256,384]{2,1,0:T(8,128)(2,1)S(1)}, u32[]{:S(2)}, u32[]{:S(2)}) collective-permute-start(bf16[2,256,384]{2,1,0:T(8,128)(2,1)S(1)} %get-tuple-element.42), channel_id=1, source_target_pairs={{0,2},{1,3},{2,0},{3,1},{4,6},{5,7},{6,4},{7,5},{8,10},{9,11},{10,... | collective-permute-start | bytes 1179656 | tf_op jit(solution)/shard_map/ppermute | solution.py:402
  51.7 0.0 collective-permute-done.15.refs_15_
  51.7 0.0 collective-permute-done.14.refs_14_
  51.7 4.2 %av.1 = (bf16[256,384]{1,0:T(8,128)(2,1)S(1)}, bf16[256,384]{1,0:T(8,128)(2,1)S(1)}, bf16[2,256,384]{2,1,0:T(8,128)(2,1)S(1)}, bf16[4,2,32,384]{3,2,1,0:T(8,128)...) custom-call(s32[2,512]{1,0:T(2,128)S(1)} %bitcast.4, ...), custom_call_target="tpu_custom_call" | custom-call | flops 905969664 | bytes 5000000 | tf_op jit(solution)/shard_map/av/pallas_call | solution.py:424
  55.9 0.1 collective-permute-start.17
  56.0 0.3 collective-permute-start.18
  56.3 3.0 %collective-permute-start.20 = (bf16[4,2,32,384]{3,2,1,0:T(8,128)(2,1)S(1)}, bf16[4,2,32,384]{3,2,1,0:T(8,128)(2,1)S(1)}, u32[]{:S(2)}, u32[]{:S(2)}) collective-permute-start(bf16[4,2,32,384]{3,2,1,0:T(8,128)(2,1)S(1)} %get-tuple-element.49), channel_id=1, source_target_pairs={{0,5},{1,4},{2,7},{3,6},{4,1},{5,0},{6,3},{7,2},{8,13},{9,12},{10,... | collective-permute-start | bytes 589832 | tf_op jit(solution)/shard_map/ppermute | solution.py:402
  59.3 5.0 %collective-permute-start.21 = (bf16[4,2,32,384]{3,2,1,0:T(8,128)(2,1)S(1)}, bf16[4,2,32,384]{3,2,1,0:T(8,128)(2,1)S(1)}, u32[]{:S(2)}, u32[]{:S(2)}) collective-permute-start(bf16[4,2,32,384]{3,2,1,0:T(8,128)(2,1)S(1)} %get-tuple-element.50), channel_id=1, source_target_pairs={{4,8},{5,9},{6,10},{7,11},{8,4},{9,5},{10,6},{11,7},{12,16},{13,17... | collective-permute-start | bytes 589832 | tf_op jit(solution)/shard_map/ppermute | solution.py:402
  64.3 3.5 %collective-permute-start.22 = (bf16[4,2,32,384]{3,2,1,0:T(8,128)(2,1)S(1)}, bf16[4,2,32,384]{3,2,1,0:T(8,128)(2,1)S(1)}, u32[]{:S(2)}, u32[]{:S(2)}) collective-permute-start(bf16[4,2,32,384]{3,2,1,0:T(8,128)(2,1)S(1)} %get-tuple-element.51), channel_id=1, source_target_pairs={{4,9},{5,8},{6,11},{7,10},{8,5},{9,4},{10,7},{11,6},{12,17},{13,16... | collective-permute-start | bytes 589832 | tf_op jit(solution)/shard_map/ppermute | solution.py:402
  67.9 1.3 %join_video.1 = (bf16[256,768]{1,0:T(8,128)(2,1)}, bf16[256,768]{1,0:T(8,128)(2,1)}, bf16[256,768]{1,0:T(8,128)(2,1)}, bf16[256,768]{1,0:T(8,128)(2,1)}, f32[8,128]{1,0:T(8,128)S(1)}) custom-call(bf16[256,384]{1,0:T(8,128)(2,1)S(1)} %get-tuple-element.37.refs_0_, bf16[256,384]{1,0:T(8,128)(2,1)S(1)} %get-tuple-element.38.refs_1_, ...), custom_call_target="tpu_custom_call" | custom-call | bytes 1600000 | tf_op jit(solution)/shard_map/join_video/pallas_call | solution.py:424
  69.2 1.5 %collective-permute-done.21.by_b = bf16[4,2,32,384]{3,2,1,0:T(8,128)(2,1)S(1)} collective-permute-done((bf16[4,2,32,384]{3,2,1,0:T(8,128)(2,1)S(1)}, bf16[4,2,32,384]{3,2,1,0:T(8,128)(2,1)S(1)}, u32[]{:S(2)}, u32[]{:S(2)}) %collective-permute-start.21) | collective-permute-done | bytes 196640 | tf_op jit(solution)/shard_map/ppermute | solution.py:402
  70.6 6.3 %collective-permute-done.22.by_bx = bf16[4,2,32,384]{3,2,1,0:T(8,128)(2,1)S(1)} collective-permute-done((bf16[4,2,32,384]{3,2,1,0:T(8,128)(2,1)S(1)}, bf16[4,2,32,384]{3,2,1,0:T(8,128)(2,1)S(1)}, u32[]{:S(2)}, u32[]{:S(2)}) %collective-permute-start.22) | collective-permute-done | bytes 196640 | tf_op jit(solution)/shard_map/ppermute | solution.py:402
  76.9 0.2 sum_audio.1
  77.1 2.2 %collective-permute-start.23 = (bf16[4,2,32,384]{3,2,1,0:T(8,128)(2,1)S(1)}, bf16[4,2,32,384]{3,2,1,0:T(8,128)(2,1)S(1)}, u32[]{:S(2)}, u32[]{:S(2)}) collective-permute-start(bf16[4,2,32,384]{3,2,1,0:T(8,128)(2,1)S(1)} %get-tuple-element.54), channel_id=1, source_target_pairs={{0,2},{1,3},{2,0},{3,1},{4,6},{5,7},{6,4},{7,5},{8,10},{9,11},{10,... | collective-permute-start | bytes 589832 | tf_op jit(solution)/shard_map/ppermute | solution.py:402
  79.2 1.1 %collective-permute-done.23.other = bf16[4,2,32,384]{3,2,1,0:T(8,128)(2,1)S(1)} collective-permute-done((bf16[4,2,32,384]{3,2,1,0:T(8,128)(2,1)S(1)}, bf16[4,2,32,384]{3,2,1,0:T(8,128)(2,1)S(1)}, u32[]{:S(2)}, u32[]{:S(2)}) %collective-permute-start.23) | collective-permute-done | bytes 196640 | tf_op jit(solution)/shard_map/ppermute | solution.py:402
  80.3 0.8 join_audio.1
  (21 shorter events, 0.0 us)
Async XLA Ops:
  0.6 3.0 %copy-start.3 = (s32[128]{0:T(128)S(1)}, s32[128]{0:T(128)}, u32[]{:S(2)}) copy-start(s32[128]{0:T(128)} %len_ref.3) | copy-start | bytes 1540
  0.6 3.0 %collective-permute-start = (bf16[32,1536]{1,0:T(8,128)(2,1)}, bf16[32,1536]{1,0:T(8,128)(2,1)S(1)}, u32[]{:S(2)}, u32[]{:S(2)}) collective-permute-start(bf16[32,1536]{1,0:T(8,128)(2,1)} %refs_0_.1), channel_id=1, source_target_pairs={{0,2},{1,3},{2,0},{3,1},{4,6},{5,7},{6,4},{7,5},{8,10},{9,11},{10,... | collective-permute-start | bytes 294920 | tf_op jit(solution)/shard_map/ppermute | solution.py:402
  1.4 2.2 %collective-permute-start.2 = (bf16[32,1536]{1,0:T(8,128)(2,1)}, bf16[32,1536]{1,0:T(8,128)(2,1)S(1)}, u32[]{:S(2)}, u32[]{:S(2)}) collective-permute-start(bf16[32,1536]{1,0:T(8,128)(2,1)} %refs_2_.1), channel_id=1, source_target_pairs={{0,2},{1,3},{2,0},{3,1},{4,6},{5,7},{6,4},{7,5},{8,10},{9,11},{10,... | collective-permute-start | bytes 294920 | tf_op jit(solution)/shard_map/ppermute | solution.py:402
  1.5 2.1 %collective-permute-start.3 = (bf16[32,1536]{1,0:T(8,128)(2,1)}, bf16[32,1536]{1,0:T(8,128)(2,1)S(1)}, u32[]{:S(2)}, u32[]{:S(2)}) collective-permute-start(bf16[32,1536]{1,0:T(8,128)(2,1)} %refs_3_.2), channel_id=1, source_target_pairs={{0,2},{1,3},{2,0},{3,1},{4,6},{5,7},{6,4},{7,5},{8,10},{9,11},{10,... | collective-permute-start | bytes 294920 | tf_op jit(solution)/shard_map/ppermute | solution.py:402
  1.9 1.7 %collective-permute-start.1 = (bf16[32,1536]{1,0:T(8,128)(2,1)}, bf16[32,1536]{1,0:T(8,128)(2,1)S(1)}, u32[]{:S(2)}, u32[]{:S(2)}) collective-permute-start(bf16[32,1536]{1,0:T(8,128)(2,1)} %refs_1_.1), channel_id=1, source_target_pairs={{0,2},{1,3},{2,0},{3,1},{4,6},{5,7},{6,4},{7,5},{8,10},{9,11},{10,... | collective-permute-start | bytes 294920 | tf_op jit(solution)/shard_map/ppermute | solution.py:402
  2.0 21.6 %collective-permute-start.11 = (bf16[256,768]{1,0:T(8,128)(2,1)}, bf16[256,768]{1,0:T(8,128)(2,1)S(1)}, u32[]{:S(2)}, u32[]{:S(2)}) collective-permute-start(bf16[256,768]{1,0:T(8,128)(2,1)} %refs_7_.3), channel_id=1, source_target_pairs={{0,2},{1,3},{2,0},{3,1},{4,6},{5,7},{6,4},{7,5},{8,10},{9,11},{10,... | collective-permute-start | bytes 1179656 | tf_op jit(solution)/shard_map/ppermute | solution.py:402
  2.4 13.7 %copy-start.4 = (bf16[256,768]{1,0:T(8,128)(2,1)S(1)}, bf16[256,768]{1,0:T(8,128)(2,1)}, u32[]{:S(2)}) copy-start(bf16[256,768]{1,0:T(8,128)(2,1)} %refs_6_.2) | copy-start | bytes 1179652
  2.4 14.7 %copy-start.5 = (bf16[256,768]{1,0:T(8,128)(2,1)S(1)}, bf16[256,768]{1,0:T(8,128)(2,1)}, u32[]{:S(2)}) copy-start(bf16[256,768]{1,0:T(8,128)(2,1)} %refs_7_.2) | copy-start | bytes 1179652
  3.6 3.8 %copy-start.1 = (bf16[256,768]{1,0:T(8,128)(2,1)S(1)}, bf16[256,768]{1,0:T(8,128)(2,1)}, u32[]{:S(2)}) copy-start(bf16[256,768]{1,0:T(8,128)(2,1)} %refs_8_.1) | copy-start | bytes 1179652
  3.6 23.4 %copy-start = (bf16[256,768]{1,0:T(8,128)(2,1)S(1)}, bf16[256,768]{1,0:T(8,128)(2,1)}, u32[]{:S(2)}) copy-start(bf16[256,768]{1,0:T(8,128)(2,1)} %refs_7_.3) | copy-start | bytes 1179652
  4.3 22.7 %copy-start.2 = (s32[512,2]{0,1:T(2,128)S(1)}, s32[512,2]{0,1:T(2,128)}, u32[]{:S(2)}) copy-start(s32[512,2]{0,1:T(2,128)} %param.18) | copy-start | bytes 12292
  4.3 11.9 %collective-permute-start.6 = (bf16[4,2,32,384]{3,2,1,0:T(8,128)(2,1)S(1)}, bf16[4,2,32,384]{3,2,1,0:T(8,128)(2,1)S(1)}, u32[]{:S(2)}, u32[]{:S(2)}) collective-permute-start(bf16[4,2,32,384]{3,2,1,0:T(8,128)(2,1)S(1)} %get-tuple-element.36), channel_id=1, source_target_pairs={{0,5},{1,4},{2,7},{3,6},{4,1},{5,0},{6,3},{7,2},{8,13},{9,12},{10,... | collective-permute-start | bytes 589832 | tf_op jit(solution)/shard_map/ppermute | solution.py:402
  6.8 10.3 %collective-permute-start.4 = (bf16[4,2,32,384]{3,2,1,0:T(8,128)(2,1)S(1)}, bf16[4,2,32,384]{3,2,1,0:T(8,128)(2,1)S(1)}, u32[]{:S(2)}, u32[]{:S(2)}) collective-permute-start(bf16[4,2,32,384]{3,2,1,0:T(8,128)(2,1)S(1)} %get-tuple-element.36), channel_id=1, source_target_pairs={{0,1},{1,0},{2,3},{3,2},{4,5},{5,4},{6,7},{7,6},{8,9},{9,8},{10,11... | collective-permute-start | bytes 589832 | tf_op jit(solution)/shard_map/ppermute | solution.py:402
  7.4 19.6 %collective-permute-start.12 = (bf16[256,768]{1,0:T(8,128)(2,1)S(1)}, bf16[256,768]{1,0:T(8,128)(2,1)S(1)}, u32[]{:S(2)}, u32[]{:S(2)}) collective-permute-start(bf16[256,768]{1,0:T(8,128)(2,1)S(1)} %copy-done.1), channel_id=1, source_target_pairs={{0,2},{1,3},{2,0},{3,1},{4,6},{5,7},{6,4},{7,5},{8,10},{9,11},{10,... | collective-permute-start | bytes 1179656 | tf_op jit(solution)/shard_map/ppermute | solution.py:402
  8.0 9.2 %collective-permute-start.5 = (bf16[4,2,32,384]{3,2,1,0:T(8,128)(2,1)S(1)}, bf16[4,2,32,384]{3,2,1,0:T(8,128)(2,1)S(1)}, u32[]{:S(2)}, u32[]{:S(2)}) collective-permute-start(bf16[4,2,32,384]{3,2,1,0:T(8,128)(2,1)S(1)} %get-tuple-element.35.refs_0_.refs_1_), channel_id=1, source_target_pairs={{0,4},{1,5},{2,6},{3,7},{4,0},{5,1},{6,2},{7,3},{8,12},{9,13},{10,... | collective-permute-start | bytes 589832 | tf_op jit(solution)/shard_map/ppermute | solution.py:402
  16.1 27.0 %collective-permute-start.9 = (bf16[256,768]{1,0:T(8,128)(2,1)S(1)}, bf16[256,768]{1,0:T(8,128)(2,1)S(1)}, u32[]{:S(2)}, u32[]{:S(2)}) collective-permute-start(bf16[256,768]{1,0:T(8,128)(2,1)S(1)} %copy-done.4), channel_id=1, source_target_pairs={{0,2},{1,3},{2,0},{3,1},{4,6},{5,7},{6,4},{7,5},{8,10},{9,11},{10,... | collective-permute-start | bytes 1179656 | tf_op jit(solution)/shard_map/ppermute | solution.py:402
  17.1 26.1 %collective-permute-start.10 = (bf16[256,768]{1,0:T(8,128)(2,1)S(1)}, bf16[256,768]{1,0:T(8,128)(2,1)S(1)}, u32[]{:S(2)}, u32[]{:S(2)}) collective-permute-start(bf16[256,768]{1,0:T(8,128)(2,1)S(1)} %copy-done.5), channel_id=1, source_target_pairs={{0,2},{1,3},{2,0},{3,1},{4,6},{5,7},{6,4},{7,5},{8,10},{9,11},{10,... | collective-permute-start | bytes 1179656 | tf_op jit(solution)/shard_map/ppermute | solution.py:402
  17.2 13.3 %collective-permute-start.8 = (bf16[4,2,32,384]{3,2,1,0:T(8,128)(2,1)S(1)}, bf16[4,2,32,384]{3,2,1,0:T(8,128)(2,1)S(1)}, u32[]{:S(2)}, u32[]{:S(2)}) collective-permute-start(bf16[4,2,32,384]{3,2,1,0:T(8,128)(2,1)S(1)} %get-tuple-element.36), channel_id=1, source_target_pairs={{4,9},{5,8},{6,11},{7,10},{8,5},{9,4},{10,7},{11,6},{12,17},{13,16... | collective-permute-start | bytes 589832 | tf_op jit(solution)/shard_map/ppermute | solution.py:402
  23.6 11.8 %collective-permute-start.7 = (bf16[4,2,32,384]{3,2,1,0:T(8,128)(2,1)S(1)}, bf16[4,2,32,384]{3,2,1,0:T(8,128)(2,1)S(1)}, u32[]{:S(2)}, u32[]{:S(2)}) collective-permute-start(bf16[4,2,32,384]{3,2,1,0:T(8,128)(2,1)S(1)} %get-tuple-element.35.refs_0_.refs_1_), channel_id=1, source_target_pairs={{4,8},{5,9},{6,10},{7,11},{8,4},{9,5},{10,6},{11,7},{12,16},{13,17... | collective-permute-start | bytes 589832 | tf_op jit(solution)/shard_map/ppermute | solution.py:402
  29.0 6.4 %collective-permute-start.13 = (f32[3,8,256]{2,1,0:T(8,128)S(1)}, f32[3,8,256]{2,1,0:T(8,128)S(1)}, u32[]{:S(2)}, u32[]{:S(2)}) collective-permute-start(f32[3,8,256]{2,1,0:T(8,128)S(1)} %stats_a.1.refs_7_.refs_11_), channel_id=1, source_target_pairs={{0,4},{1,5},{2,6},{3,7},{4,0},{5,1},{6,2},{7,3},{8,12},{9,13},{10,... | collective-permute-start | bytes 73736 | tf_op jit(solution)/shard_map/ppermute | solution.py:402
  36.9 14.7 %collective-permute-start.15 = (f32[3,8,256]{2,1,0:T(8,128)S(1)}, f32[3,8,256]{2,1,0:T(8,128)S(1)}, u32[]{:S(2)}, u32[]{:S(2)}) collective-permute-start(f32[3,8,256]{2,1,0:T(8,128)S(1)} %stats_b.1.refs_12_), channel_id=1, source_target_pairs={{4,12},{5,13},{6,14},{7,15},{8,0},{9,1},{10,2},{11,3},{12,20},{13,... | collective-permute-start | bytes 73736 | tf_op jit(solution)/shard_map/ppermute | solution.py:402
  38.9 12.8 %collective-permute-start.14 = (f32[3,8,256]{2,1,0:T(8,128)S(1)}, f32[3,8,256]{2,1,0:T(8,128)S(1)}, u32[]{:S(2)}, u32[]{:S(2)}) collective-permute-start(f32[3,8,256]{2,1,0:T(8,128)S(1)} %stats_b.1.refs_12_), channel_id=1, source_target_pairs={{4,8},{5,9},{6,10},{7,11},{8,4},{9,5},{10,6},{11,7},{12,16},{13,17... | collective-permute-start | bytes 73736 | tf_op jit(solution)/shard_map/ppermute | solution.py:402
  47.4 11.9 %collective-permute-start.16 = (bf16[2,256,384]{2,1,0:T(8,128)(2,1)S(1)}, bf16[2,256,384]{2,1,0:T(8,128)(2,1)S(1)}, u32[]{:S(2)}, u32[]{:S(2)}) collective-permute-start(bf16[2,256,384]{2,1,0:T(8,128)(2,1)S(1)} %get-tuple-element.42), channel_id=1, source_target_pairs={{0,2},{1,3},{2,0},{3,1},{4,6},{5,7},{6,4},{7,5},{8,10},{9,11},{10,... | collective-permute-start | bytes 1179656 | tf_op jit(solution)/shard_map/ppermute | solution.py:402
  55.9 8.5 %collective-permute-start.17 = (bf16[2,256,384]{2,1,0:T(8,128)(2,1)S(1)}, bf16[2,256,384]{2,1,0:T(8,128)(2,1)S(1)}, u32[]{:S(2)}, u32[]{:S(2)}) collective-permute-start(bf16[2,256,384]{2,1,0:T(8,128)(2,1)S(1)} %get-tuple-element.43), channel_id=1, source_target_pairs={{0,2},{1,3},{2,0},{3,1},{4,6},{5,7},{6,4},{7,5},{8,10},{9,11},{10,... | collective-permute-start | bytes 1179656 | tf_op jit(solution)/shard_map/ppermute | solution.py:402
  56.0 13.2 %collective-permute-start.18 = (bf16[4,2,32,384]{3,2,1,0:T(8,128)(2,1)S(1)}, bf16[4,2,32,384]{3,2,1,0:T(8,128)(2,1)S(1)}, u32[]{:S(2)}, u32[]{:S(2)}) collective-permute-start(bf16[4,2,32,384]{3,2,1,0:T(8,128)(2,1)S(1)} %get-tuple-element.47), channel_id=1, source_target_pairs={{0,1},{1,0},{2,3},{3,2},{4,5},{5,4},{6,7},{7,6},{8,9},{9,8},{10,11... | collective-permute-start | bytes 589832 | tf_op jit(solution)/shard_map/ppermute | solution.py:402
  56.3 12.9 %collective-permute-start.19 = (bf16[4,2,32,384]{3,2,1,0:T(8,128)(2,1)S(1)}, bf16[4,2,32,384]{3,2,1,0:T(8,128)(2,1)S(1)}, u32[]{:S(2)}, u32[]{:S(2)}) collective-permute-start(bf16[4,2,32,384]{3,2,1,0:T(8,128)(2,1)S(1)} %get-tuple-element.48), channel_id=1, source_target_pairs={{0,4},{1,5},{2,6},{3,7},{4,0},{5,1},{6,2},{7,3},{8,12},{9,13},{10,... | collective-permute-start | bytes 589832 | tf_op jit(solution)/shard_map/ppermute | solution.py:402
  56.3 12.9 %collective-permute-start.20 = (bf16[4,2,32,384]{3,2,1,0:T(8,128)(2,1)S(1)}, bf16[4,2,32,384]{3,2,1,0:T(8,128)(2,1)S(1)}, u32[]{:S(2)}, u32[]{:S(2)}) collective-permute-start(bf16[4,2,32,384]{3,2,1,0:T(8,128)(2,1)S(1)} %get-tuple-element.49), channel_id=1, source_target_pairs={{0,5},{1,4},{2,7},{3,6},{4,1},{5,0},{6,3},{7,2},{8,13},{9,12},{10,... | collective-permute-start | bytes 589832 | tf_op jit(solution)/shard_map/ppermute | solution.py:402
  59.3 11.3 %collective-permute-start.21 = (bf16[4,2,32,384]{3,2,1,0:T(8,128)(2,1)S(1)}, bf16[4,2,32,384]{3,2,1,0:T(8,128)(2,1)S(1)}, u32[]{:S(2)}, u32[]{:S(2)}) collective-permute-start(bf16[4,2,32,384]{3,2,1,0:T(8,128)(2,1)S(1)} %get-tuple-element.50), channel_id=1, source_target_pairs={{4,8},{5,9},{6,10},{7,11},{8,4},{9,5},{10,6},{11,7},{12,16},{13,17... | collective-permute-start | bytes 589832 | tf_op jit(solution)/shard_map/ppermute | solution.py:402
  64.3 12.6 %collective-permute-start.22 = (bf16[4,2,32,384]{3,2,1,0:T(8,128)(2,1)S(1)}, bf16[4,2,32,384]{3,2,1,0:T(8,128)(2,1)S(1)}, u32[]{:S(2)}, u32[]{:S(2)}) collective-permute-start(bf16[4,2,32,384]{3,2,1,0:T(8,128)(2,1)S(1)} %get-tuple-element.51), channel_id=1, source_target_pairs={{4,9},{5,8},{6,11},{7,10},{8,5},{9,4},{10,7},{11,6},{12,17},{13,16... | collective-permute-start | bytes 589832 | tf_op jit(solution)/shard_map/ppermute | solution.py:402
  77.1 3.2 %collective-permute-start.23 = (bf16[4,2,32,384]{3,2,1,0:T(8,128)(2,1)S(1)}, bf16[4,2,32,384]{3,2,1,0:T(8,128)(2,1)S(1)}, u32[]{:S(2)}, u32[]{:S(2)}) collective-permute-start(bf16[4,2,32,384]{3,2,1,0:T(8,128)(2,1)S(1)} %get-tuple-element.54), channel_id=1, source_target_pairs={{0,2},{1,3},{2,0},{3,1},{4,6},{5,7},{6,4},{7,5},{8,10},{9,11},{10,... | collective-permute-start | bytes 589832 | tf_op jit(solution)/shard_map/ppermute | solution.py:402
